TPU v7x, 256 devices: a whole 4x4x8 slice. The times are simulated.
256 devices in a mesh: row: 32 (over x_lo, z, core), col: 8 (over y, x_hi).
Axes of the slice: x: 4 (x_hi: 2, x_lo: 2; x = x_hi * 2 + x_lo), y: 4, z: 8, core: 2. Of those that a mesh axis runs over, the one named last changes fastest.
Arguments:
- covariance: float32 [16384, 16384], P('row', 'col'), may hold values from -6 to 6
- lon_courant: float32 [128, 128], replicated, may hold values from 0.05 to 0.95
- lat_courant: float32 [128, 128], replicated, may hold values from 0.05 to 0.9
- zonal_upwind_sign: int32 [128, 128], replicated, may hold values 0 or 1
- lat_sign: int32 [128, 128], replicated, may hold values 0 or 1
- cycle_counts: int32 [128], replicated, may hold values from 1 to 4
Outputs:
- forecast: float32 [16384, 16384], P('row', 'col')
Inputs may be any that keep to these rules, and one draw needn't show every extreme that they name: `zonal_upwind_sign`: 1 where the wind blows toward growing longitude, 0 otherwise. `lat_sign`: 1 where the wind blows toward growing latitude, 0 otherwise.
All inputs are finite; a program needn't handle non-finite values.
Results may differ from a plain program's by a relative error of at most 0.00002.
Values sent between devices are 32-bit elements; how exact they have to be, the bound alone decides.
A program may use at most 128 MiB of HBM per device.

v0:
```python
import jax
import jax.numpy as jnp
from jax import lax
from jax.sharding import PartitionSpec as P

NLON = 128
SUBCYCLES = 4


def extended(block, sides, width):
    for axis, dim in sides:
        count = lax.axis_size(axis)
        forward = [(i, i + 1) for i in range(count - 1)]
        backward = [(target, source) for source, target in forward]
        low = lax.ppermute(
            lax.slice_in_dim(block, block.shape[dim] - width, None, axis=dim), axis, forward
        )
        high = lax.ppermute(lax.slice_in_dim(block, 0, width, axis=dim), axis, backward)
        block = jnp.concatenate([low, block, high], axis=dim)
    return block


def shape_for(table_rows, lat_axis):
    if lat_axis == 0:
        return table_rows[:, :, None]
    return table_rows[None, :, :]


def lat_update(widened, courant, upwind_sign, lat_axis):
    extent = widened.shape[lat_axis]
    below_cells = lax.slice_in_dim(widened, 0, extent - 2, axis=lat_axis)
    center = lax.slice_in_dim(widened, 1, extent - 1, axis=lat_axis)
    above_cells = lax.slice_in_dim(widened, 2, extent, axis=lat_axis)
    nearby = jnp.where(upwind_sign == 1, below_cells, above_cells)
    return center - courant * (center - nearby)


def lon_sweep(values, lon_rate, zonal_heading, counts, lon_axis):

    def subcycle(cycle_index, current):
        cell_rate = jnp.where(cycle_index < counts, lon_rate, jnp.zeros_like(lon_rate))
        western_neighbour = jnp.roll(current, 1, axis=lon_axis)
        east_cell = jnp.roll(current, -1, axis=lon_axis)
        nearby = jnp.where(zonal_heading == 1, western_neighbour, east_cell)
        return current - cell_rate * (current - nearby)

    return lax.fori_loop(0, SUBCYCLES, subcycle, values)


def advance(values, first_lat, lat_axis, lon_axis, tables, fetch):
    lats_here = values.shape[lat_axis]
    picked = []
    for table_rows in tables:
        window = lax.dynamic_slice_in_dim(table_rows, first_lat + 2, lats_here, 0)
        picked.append(shape_for(window, lat_axis))
    middle = lat_update(fetch(values, 1), picked[1], picked[3], lat_axis)
    middle = lon_sweep(middle, picked[0], picked[2], picked[4], lon_axis)
    return lat_update(fetch(middle, 1), picked[1], picked[3], lat_axis)


def per_device(covariance, lon_courant, lat_courant, zonal_upwind_sign, lat_sign, cycle_counts):
    tables = tuple(
        (
            jnp.pad(table_rows, ((2, 2), (0, 0)))
            for table_rows in (
                lon_courant,
                lat_courant,
                zonal_upwind_sign,
                lat_sign,
                cycle_counts[:, None],
            )
        )
    )
    row_extent, col_extent = covariance.shape
    row_lats = row_extent // NLON
    col_lats = col_extent // NLON

    def row_gather(values, layers):
        return extended(values, (("row", 0),), 1)

    def col_fetch(values, layers):
        return extended(values, (("col", 1),), 1)

    row_start = lax.axis_index("row") * row_lats
    col_start = lax.axis_index("col") * col_lats
    columns_moved = advance(
        covariance.reshape(row_lats, NLON, col_extent), row_start, 0, 1, tables, row_gather
    )
    advanced = columns_moved.reshape(row_extent, col_extent)
    rows_moved = advance(
        advanced.reshape(row_extent, col_lats, NLON), col_start, 1, 2, tables, col_fetch
    )
    return rows_moved.reshape(row_extent, col_extent)


def solution(mesh):
    placed = (P("row", "col"), P(), P(), P(), P(), P())
    return jax.shard_map(
        per_device, mesh=mesh, in_specs=placed, out_specs=P("row", "col"), check_vma=False
    )
```

profile of v0, /device:TPU:103, one launch (start us, length us, event | category | flops | bytes accessed | tf_op | source)
XLA Modules:
  0.0 192.5 jit_solution(8706882976734498191)
XLA Ops:
  0.0 2.8 %slice_bitcast_fusion.1 = (f32[1,128,2048]{2,1,0:T(8,128)}, f32[1,128,2048]{2,1,0:T(8,128)S(1)}) fusion(f32[512,2048]{1,0:T(8,128)} %param.10), kind=kLoop, calls=%fused_computation.40 | loop fusion | bytes 4194304 | tf_op jit(solution)/shard_map/slice | solution.py:16
  2.8 5.3 %collective-permute-start = (f32[1,128,2048]{2,1,0:T(8,128)}, f32[1,128,2048]{2,1,0:T(8,128)S(1)}, u32[]{:S(2)}, u32[]{:S(2)}) collective-permute-start(f32[1,128,2048]{2,1,0:T(8,128)} %get-tuple-element.229), channel_id=1, source_target_pairs={{0,8},{8,16},{16,24},{24,32},{32,40},{40,48},{48,56},{56,64},{64,7... | collective-permute-start | bytes 3145736 | tf_op jit(solution)/shard_map/ppermute | solution.py:15
  8.1 1.9 collective-permute-start.1
  10.1 0.1 fusion.28
  10.2 9.9 %collective-permute-done = f32[1,128,2048]{2,1,0:T(8,128)S(1)} collective-permute-done((f32[1,128,2048]{2,1,0:T(8,128)}, f32[1,128,2048]{2,1,0:T(8,128)S(1)}, u32[]{:S(2)}, u32[]{:S(2)}) %collective-permute-start) | collective-permute-done | bytes 1048608 | tf_op jit(solution)/shard_map/ppermute | solution.py:15
  20.1 5.3 %collective-permute-done.1 = f32[1,128,2048]{2,1,0:T(8,128)S(1)} collective-permute-done((f32[1,128,2048]{2,1,0:T(8,128)S(1)}, f32[1,128,2048]{2,1,0:T(8,128)S(1)}, u32[]{:S(2)}, u32[]{:S(2)}) %collective-permute-start.1) | collective-permute-done | bytes 1048608 | tf_op jit(solution)/shard_map/ppermute | solution.py:18
  25.4 6.2 %fusion.21 = f32[4,128,2048]{2,1,0:T(8,128)} fusion(f32[4,128,2048]{2,1,0:T(8,128)} %bitcast.53, f32[1,128,2048]{2,1,0:T(8,128)S(1)} %collective-permute-done.1, f32[1,128,2048]{2,1,0:T(8,128)S(1)} %collective-permute-done, f32[4,128]{1,0:T(4,128)S(1)} %pad_dynamic-slice_fusion.7, pred[4,128]{1,0:T(4,128)(4,1)S(1)} %fusion.27), kind=kLoop, calls=%fused_computation.37 | loop fusion | flops 6291456 | bytes 10488320 | tf_op jit(solution)/shard_map/sub | solution.py:35
  31.6 37.5 %while.26 = (s32[]{:T(128)}, f32[4,128,2048]{2,1,0:T(8,128)}, s32[4,1,1]{0,2,1:T(1,128)S(1)}, f32[4,128,1]{1,0,2:T(4,128)S(1)}, s32[4,128,1]{1,0,2:T(4,128)S(1)}, /*index=5*/s32[]{:T(128)}) while((s32[]{:T(128)}, f32[4,128,2048]{2,1,0:T(8,128)}, s32[4,1,1]{0,2,1:T(1,128)S(1)}, f32[4,128,1]{1,0,2:T(4,128)S(1)}, s32[4,128,1]{1,0,2:T(4,128)S(1)}, ...), condition=%wide.region_1.2_spmd, body=%wide.region_0.1_spmd.sunk | while | flops 6292486 | bytes 67118240 | solution.py:47
  31.7 1.1 fusion.44
  32.8 4.6 %fusion.43 = (f32[4,127,2048]{2,1,0:T(8,128)S(1)}, f32[4,127,2048]{2,1,0:T(8,128)S(1)}) fusion(f32[4,128,2048]{2,1,0:T(8,128)} %get-tuple-element.316), kind=kLoop, calls=%fused_computation.59.clone.1 | loop fusion | bytes 16646144 | tf_op jit(solution)/shard_map/while/body/eval_jaxpr/jit(_roll_static)/slice | solution.py:43
  37.5 1.5 fusion.45
  39.0 2.0 %copy-done.3 = f32[4,128,2048]{2,1,0:T(8,128)} copy-done((f32[4,128,2048]{2,1,0:T(8,128)}, f32[4,128,2048]{2,1,0:T(8,128)S(1)}, u32[]{:S(2)}) %copy-start.3) | copy-done | bytes 4194328 | tf_op jit(solution)/shard_map/while
  41.1 1.1 fusion.44
  42.2 4.6 %fusion.43 = (f32[4,127,2048]{2,1,0:T(8,128)S(1)}, f32[4,127,2048]{2,1,0:T(8,128)S(1)}) fusion(f32[4,128,2048]{2,1,0:T(8,128)} %get-tuple-element.316), kind=kLoop, calls=%fused_computation.59.clone.1 | loop fusion | bytes 16646144 | tf_op jit(solution)/shard_map/while/body/eval_jaxpr/jit(_roll_static)/slice | solution.py:43
  46.8 1.5 fusion.45
  48.4 2.0 %copy-done.3 = f32[4,128,2048]{2,1,0:T(8,128)} copy-done((f32[4,128,2048]{2,1,0:T(8,128)}, f32[4,128,2048]{2,1,0:T(8,128)S(1)}, u32[]{:S(2)}) %copy-start.3) | copy-done | bytes 4194328 | tf_op jit(solution)/shard_map/while
  50.5 1.1 fusion.44
  51.6 4.6 %fusion.43 = (f32[4,127,2048]{2,1,0:T(8,128)S(1)}, f32[4,127,2048]{2,1,0:T(8,128)S(1)}) fusion(f32[4,128,2048]{2,1,0:T(8,128)} %get-tuple-element.316), kind=kLoop, calls=%fused_computation.59.clone.1 | loop fusion | bytes 16646144 | tf_op jit(solution)/shard_map/while/body/eval_jaxpr/jit(_roll_static)/slice | solution.py:43
  56.2 1.5 fusion.45
  57.8 2.0 %copy-done.3 = f32[4,128,2048]{2,1,0:T(8,128)} copy-done((f32[4,128,2048]{2,1,0:T(8,128)}, f32[4,128,2048]{2,1,0:T(8,128)S(1)}, u32[]{:S(2)}) %copy-start.3) | copy-done | bytes 4194328 | tf_op jit(solution)/shard_map/while
  59.8 1.1 fusion.44
  60.9 4.6 %fusion.43 = (f32[4,127,2048]{2,1,0:T(8,128)S(1)}, f32[4,127,2048]{2,1,0:T(8,128)S(1)}) fusion(f32[4,128,2048]{2,1,0:T(8,128)} %get-tuple-element.316), kind=kLoop, calls=%fused_computation.59.clone.1 | loop fusion | bytes 16646144 | tf_op jit(solution)/shard_map/while/body/eval_jaxpr/jit(_roll_static)/slice | solution.py:43
  65.6 1.5 fusion.45
  67.1 2.0 %copy-done.3 = f32[4,128,2048]{2,1,0:T(8,128)} copy-done((f32[4,128,2048]{2,1,0:T(8,128)}, f32[4,128,2048]{2,1,0:T(8,128)S(1)}, u32[]{:S(2)}) %copy-start.3) | copy-done | bytes 4194328 | tf_op jit(solution)/shard_map/while
  69.1 2.7 %fusion.36 = (f32[1,128,2048]{2,1,0:T(8,128)}, f32[1,128,2048]{2,1,0:T(8,128)S(1)}) fusion(f32[4,128,2048]{2,1,0:T(8,128)} %get-tuple-element.193), kind=kLoop, calls=%fused_computation.65 | loop fusion | bytes 4194304 | tf_op jit(solution)/shard_map/slice | solution.py:16
  71.9 1.9 collective-permute-start.2
  73.8 2.4 %collective-permute-start.3 = (f32[1,128,2048]{2,1,0:T(8,128)S(1)}, f32[1,128,2048]{2,1,0:T(8,128)S(1)}, u32[]{:S(2)}, u32[]{:S(2)}) collective-permute-start(f32[1,128,2048]{2,1,0:T(8,128)S(1)} %get-tuple-element.228), channel_id=1, source_target_pairs={{8,0},{16,8},{24,16},{32,24},{40,32},{48,40},{56,48},{64,56},{72,6... | collective-permute-start | bytes 3145736 | tf_op jit(solution)/shard_map/ppermute | solution.py:18
  76.3 9.6 %collective-permute-done.2 = f32[1,128,2048]{2,1,0:T(8,128)S(1)} collective-permute-done((f32[1,128,2048]{2,1,0:T(8,128)}, f32[1,128,2048]{2,1,0:T(8,128)S(1)}, u32[]{:S(2)}, u32[]{:S(2)}) %collective-permute-start.2) | collective-permute-done | bytes 1048608 | tf_op jit(solution)/shard_map/ppermute | solution.py:15
  85.8 5.3 %collective-permute-done.3 = f32[1,128,2048]{2,1,0:T(8,128)S(1)} collective-permute-done((f32[1,128,2048]{2,1,0:T(8,128)S(1)}, f32[1,128,2048]{2,1,0:T(8,128)S(1)}, u32[]{:S(2)}, u32[]{:S(2)}) %collective-permute-start.3) | collective-permute-done | bytes 1048608 | tf_op jit(solution)/shard_map/ppermute | solution.py:18
  91.1 5.0 %fusion.17 = f32[4,128,2048]{2,1,0:T(8,128)S(1)} fusion(f32[4,128,2048]{2,1,0:T(8,128)} %get-tuple-element.193, f32[1,128,2048]{2,1,0:T(8,128)S(1)} %collective-permute-done.3, f32[1,128,2048]{2,1,0:T(8,128)S(1)} %collective-permute-done.2, f32[4,128]{1,0:T(4,128)S(1)} %pad_dynamic-slice_fusion.7, pred[4,128]{1,0:T(4,128)(4,1)S(1)} %fusion.27), kind=kLoop, calls=%fused_computation.31 | loop fusion | flops 6291456 | bytes 10488320 | tf_op jit(solution)/shard_map/sub | solution.py:35
  96.1 0.9 copy.7
  97.0 0.4 fusion.35
  97.4 4.0 %collective-permute-start.4 = (f32[512,1,128]{2,1,0:T(1,128)S(1)}, f32[512,1,128]{2,1,0:T(1,128)S(1)}, u32[]{:S(2)}, u32[]{:S(2)}) collective-permute-start(f32[512,1,128]{2,1,0:T(1,128)S(1)} %get-tuple-element.225), channel_id=1, source_target_pairs={{0,1},{1,2},{2,3},{3,4},{4,5},{5,6},{6,7},{8,9},{9,10},{10,11},{11... | collective-permute-start | bytes 786440 | tf_op jit(solution)/shard_map/ppermute | solution.py:15
  101.4 2.8 %collective-permute-start.5 = (f32[512,1,128]{2,1,0:T(1,128)S(1)}, f32[512,1,128]{2,1,0:T(1,128)S(1)}, u32[]{:S(2)}, u32[]{:S(2)}) collective-permute-start(f32[512,1,128]{2,1,0:T(1,128)S(1)} %get-tuple-element.226), channel_id=1, source_target_pairs={{1,0},{2,1},{3,2},{4,3},{5,4},{6,5},{7,6},{9,8},{10,9},{11,10},{12... | collective-permute-start | bytes 786440 | tf_op jit(solution)/shard_map/ppermute | solution.py:18
  104.2 0.1 fusion.29
  104.3 3.2 %collective-permute-done.4 = f32[512,1,128]{2,1,0:T(1,128)S(1)} collective-permute-done((f32[512,1,128]{2,1,0:T(1,128)S(1)}, f32[512,1,128]{2,1,0:T(1,128)S(1)}, u32[]{:S(2)}, u32[]{:S(2)}) %collective-permute-start.4) | collective-permute-done | bytes 262176 | tf_op jit(solution)/shard_map/ppermute | solution.py:15
  107.5 5.8 %collective-permute-done.5 = f32[512,1,128]{2,1,0:T(1,128)S(1)} collective-permute-done((f32[512,1,128]{2,1,0:T(1,128)S(1)}, f32[512,1,128]{2,1,0:T(1,128)S(1)}, u32[]{:S(2)}, u32[]{:S(2)}) %collective-permute-start.5) | collective-permute-done | bytes 262176 | tf_op jit(solution)/shard_map/ppermute | solution.py:18
  113.3 3.1 %fusion.13 = f32[512,16,128]{2,1,0:T(8,128)} fusion(f32[512,16,128]{2,1,0:T(8,128)S(1)} %bitcast.50, f32[512,1,128]{2,1,0:T(1,128)S(1)} %collective-permute-done.5, f32[512,1,128]{2,1,0:T(1,128)S(1)} %collective-permute-done.4, f32[16,128]{1,0:T(8,128)S(1)} %pad_dynamic-slice_fusion.6, pred[16,128]{1,0:T(8,128)(4,1)S(1)} %fusion.22), kind=kLoop, calls=%fused_computation.25 | loop fusion | flops 6291456 | bytes 8923136 | tf_op jit(solution)/shard_map/sub | solution.py:35
  116.4 45.1 %while.27 = (s32[]{:T(128)}, f32[512,16,128]{2,1,0:T(8,128)}, s32[1,16,1]{1,2,0:T(1,128)S(1)}, f32[1,16,128]{2,1,0:T(8,128)S(1)}, s32[1,16,128]{2,1,0:T(8,128)S(1)}, /*index=5*/s32[]{:T(128)}) while((s32[]{:T(128)}, f32[512,16,128]{2,1,0:T(8,128)}, s32[1,16,1]{1,2,0:T(1,128)S(1)}, f32[1,16,128]{2,1,0:T(8,128)S(1)}, ...), condition=%wide.region_3.4_spmd, body=%wide.region_2.3_spmd.sunk | while | flops 6295570 | bytes 67145960 | solution.py:47
  116.4 0.1 bitcast_select_fusion.5
  116.5 4.9 %fusion.47 = (f32[512,16,1]{2,1,0:T(8,128)S(1)}, f32[512,16,1]{2,1,0:T(8,128)S(1)}) fusion(f32[512,16,128]{2,1,0:T(8,128)} %get-tuple-element.334), kind=kLoop, calls=%fused_computation.62.clone.1 | loop fusion | bytes 131072 | tf_op jit(solution)/shard_map/while/body/eval_jaxpr/jit(_roll_static)/slice | solution.py:43
  121.4 1.3 fusion.46
  122.8 2.9 %fusion.48 = f32[512,16,128]{2,1,0:T(8,128)S(1)} fusion(f32[512,16,128]{2,1,0:T(8,128)S(1)} %copy-done, f32[512,16,127]{2,1,0:T(8,128)S(1)} %get-tuple-element.305, f32[512,16,1]{2,1,0:T(8,128)S(1)} %get-tuple-element.306, f32[512,16,1]{2,1,0:T(8,128)S(1)} %get-tuple-element.307, f32[512,16,127]{2,1,0:T(8,128)S(1)} %get-tuple-element.308, ...), kind=kLoop, calls=%fused_computation.10.clone.1 | loop fusion | flops 6291456 | bytes 16787456 | tf_op jit(solution)/shard_map/while/body/eval_jaxpr/sub | solution.py:45
  125.6 2.0 %copy-done.1 = f32[512,16,128]{2,1,0:T(8,128)} copy-done((f32[512,16,128]{2,1,0:T(8,128)}, f32[512,16,128]{2,1,0:T(8,128)S(1)}, u32[]{:S(2)}) %copy-start.1) | copy-done | bytes 4194328 | tf_op jit(solution)/shard_map/while
  127.7 0.1 bitcast_select_fusion.5
  127.7 4.9 %fusion.47 = (f32[512,16,1]{2,1,0:T(8,128)S(1)}, f32[512,16,1]{2,1,0:T(8,128)S(1)}) fusion(f32[512,16,128]{2,1,0:T(8,128)} %get-tuple-element.334), kind=kLoop, calls=%fused_computation.62.clone.1 | loop fusion | bytes 131072 | tf_op jit(solution)/shard_map/while/body/eval_jaxpr/jit(_roll_static)/slice | solution.py:43
  132.7 1.3 fusion.46
  134.0 2.9 %fusion.48 = f32[512,16,128]{2,1,0:T(8,128)S(1)} fusion(f32[512,16,128]{2,1,0:T(8,128)S(1)} %copy-done, f32[512,16,127]{2,1,0:T(8,128)S(1)} %get-tuple-element.305, f32[512,16,1]{2,1,0:T(8,128)S(1)} %get-tuple-element.306, f32[512,16,1]{2,1,0:T(8,128)S(1)} %get-tuple-element.307, f32[512,16,127]{2,1,0:T(8,128)S(1)} %get-tuple-element.308, ...), kind=kLoop, calls=%fused_computation.10.clone.1 | loop fusion | flops 6291456 | bytes 16787456 | tf_op jit(solution)/shard_map/while/body/eval_jaxpr/sub | solution.py:45
  136.9 2.0 %copy-done.1 = f32[512,16,128]{2,1,0:T(8,128)} copy-done((f32[512,16,128]{2,1,0:T(8,128)}, f32[512,16,128]{2,1,0:T(8,128)S(1)}, u32[]{:S(2)}) %copy-start.1) | copy-done | bytes 4194328 | tf_op jit(solution)/shard_map/while
  139.0 4.9 %fusion.47 = (f32[512,16,1]{2,1,0:T(8,128)S(1)}, f32[512,16,1]{2,1,0:T(8,128)S(1)}) fusion(f32[512,16,128]{2,1,0:T(8,128)} %get-tuple-element.334), kind=kLoop, calls=%fused_computation.62.clone.1 | loop fusion | bytes 131072 | tf_op jit(solution)/shard_map/while/body/eval_jaxpr/jit(_roll_static)/slice | solution.py:43
  144.0 1.3 fusion.46
  145.3 2.9 %fusion.48 = f32[512,16,128]{2,1,0:T(8,128)S(1)} fusion(f32[512,16,128]{2,1,0:T(8,128)S(1)} %copy-done, f32[512,16,127]{2,1,0:T(8,128)S(1)} %get-tuple-element.305, f32[512,16,1]{2,1,0:T(8,128)S(1)} %get-tuple-element.306, f32[512,16,1]{2,1,0:T(8,128)S(1)} %get-tuple-element.307, f32[512,16,127]{2,1,0:T(8,128)S(1)} %get-tuple-element.308, ...), kind=kLoop, calls=%fused_computation.10.clone.1 | loop fusion | flops 6291456 | bytes 16787456 | tf_op jit(solution)/shard_map/while/body/eval_jaxpr/sub | solution.py:45
  148.2 2.0 %copy-done.1 = f32[512,16,128]{2,1,0:T(8,128)} copy-done((f32[512,16,128]{2,1,0:T(8,128)}, f32[512,16,128]{2,1,0:T(8,128)S(1)}, u32[]{:S(2)}) %copy-start.1) | copy-done | bytes 4194328 | tf_op jit(solution)/shard_map/while
  150.3 4.9 %fusion.47 = (f32[512,16,1]{2,1,0:T(8,128)S(1)}, f32[512,16,1]{2,1,0:T(8,128)S(1)}) fusion(f32[512,16,128]{2,1,0:T(8,128)} %get-tuple-element.334), kind=kLoop, calls=%fused_computation.62.clone.1 | loop fusion | bytes 131072 | tf_op jit(solution)/shard_map/while/body/eval_jaxpr/jit(_roll_static)/slice | solution.py:43
  155.2 1.3 fusion.46
  156.6 2.9 %fusion.48 = f32[512,16,128]{2,1,0:T(8,128)S(1)} fusion(f32[512,16,128]{2,1,0:T(8,128)S(1)} %copy-done, f32[512,16,127]{2,1,0:T(8,128)S(1)} %get-tuple-element.305, f32[512,16,1]{2,1,0:T(8,128)S(1)} %get-tuple-element.306, f32[512,16,1]{2,1,0:T(8,128)S(1)} %get-tuple-element.307, f32[512,16,127]{2,1,0:T(8,128)S(1)} %get-tuple-element.308, ...), kind=kLoop, calls=%fused_computation.10.clone.1 | loop fusion | flops 6291456 | bytes 16787456 | tf_op jit(solution)/shard_map/while/body/eval_jaxpr/sub | solution.py:45
  159.5 2.0 %copy-done.1 = f32[512,16,128]{2,1,0:T(8,128)} copy-done((f32[512,16,128]{2,1,0:T(8,128)}, f32[512,16,128]{2,1,0:T(8,128)S(1)}, u32[]{:S(2)}) %copy-start.1) | copy-done | bytes 4194328 | tf_op jit(solution)/shard_map/while
  161.5 2.6 %fusion.34 = (f32[512,1,128]{2,1,0:T(1,128)S(1)}, f32[512,1,128]{2,1,0:T(1,128)S(1)}) fusion(f32[512,16,128]{2,1,0:T(8,128)} %get-tuple-element.194), kind=kLoop, calls=%fused_computation.63 | loop fusion | bytes 1048576 | tf_op jit(solution)/shard_map/slice | solution.py:16
  164.1 4.0 %collective-permute-start.6 = (f32[512,1,128]{2,1,0:T(1,128)S(1)}, f32[512,1,128]{2,1,0:T(1,128)S(1)}, u32[]{:S(2)}, u32[]{:S(2)}) collective-permute-start(f32[512,1,128]{2,1,0:T(1,128)S(1)} %get-tuple-element.223), channel_id=1, source_target_pairs={{0,1},{1,2},{2,3},{3,4},{4,5},{5,6},{6,7},{8,9},{9,10},{10,11},{11... | collective-permute-start | bytes 786440 | tf_op jit(solution)/shard_map/ppermute | solution.py:15
  168.1 2.9 %collective-permute-start.7 = (f32[512,1,128]{2,1,0:T(1,128)S(1)}, f32[512,1,128]{2,1,0:T(1,128)S(1)}, u32[]{:S(2)}, u32[]{:S(2)}) collective-permute-start(f32[512,1,128]{2,1,0:T(1,128)S(1)} %get-tuple-element.224), channel_id=1, source_target_pairs={{1,0},{2,1},{3,2},{4,3},{5,4},{6,5},{7,6},{9,8},{10,9},{11,10},{12... | collective-permute-start | bytes 786440 | tf_op jit(solution)/shard_map/ppermute | solution.py:18
  171.1 4.2 %collective-permute-done.6 = f32[512,1,128]{2,1,0:T(1,128)S(1)} collective-permute-done((f32[512,1,128]{2,1,0:T(1,128)S(1)}, f32[512,1,128]{2,1,0:T(1,128)S(1)}, u32[]{:S(2)}, u32[]{:S(2)}) %collective-permute-start.6) | collective-permute-done | bytes 262176 | tf_op jit(solution)/shard_map/ppermute | solution.py:15
  175.3 6.6 %collective-permute-done.7 = f32[512,1,128]{2,1,0:T(1,128)S(1)} collective-permute-done((f32[512,1,128]{2,1,0:T(1,128)S(1)}, f32[512,1,128]{2,1,0:T(1,128)S(1)}, u32[]{:S(2)}, u32[]{:S(2)}) %collective-permute-start.7) | collective-permute-done | bytes 262176 | tf_op jit(solution)/shard_map/ppermute | solution.py:18
  181.9 6.6 %fusion.9 = f32[512,16,128]{2,1,0:T(8,128)S(1)} fusion(f32[512,16,128]{2,1,0:T(8,128)} %get-tuple-element.194, f32[512,1,128]{2,1,0:T(1,128)S(1)} %collective-permute-done.7, f32[512,1,128]{2,1,0:T(1,128)S(1)} %collective-permute-done.6, f32[16,128]{1,0:T(8,128)S(1)} %pad_dynamic-slice_fusion.6, pred[16,128]{1,0:T(8,128)(4,1)S(1)} %fusion.22), kind=kLoop, calls=%fused_computation.19 | loop fusion | flops 6291456 | bytes 8923136 | tf_op jit(solution)/shard_map/sub | solution.py:35
  188.5 4.0 %copy.10 = f32[64,8,16,128]{3,1,2,0:T(8,128)} copy(f32[64,8,16,128]{3,2,1,0:T(8,128)S(1)} %bitcast.52) | data formatting | bytes 8388608
  (64 shorter events, 1.0 us)
Async XLA Ops:
  0.0 10.0 %copy-start.4 = (s32[128,128]{1,0:T(8,128)S(1)}, s32[128,128]{1,0:T(8,128)}, u32[]{:S(2)}) copy-start(s32[128,128]{1,0:T(8,128)} %param.14) | copy-start | bytes 196612
  0.0 10.1 %copy-start.8 = (s32[128]{0:T(128)S(1)}, s32[128]{0:T(128)}, u32[]{:S(2)}) copy-start(s32[128]{0:T(128)} %param.15) | copy-start | bytes 1540
  0.0 10.2 %copy-start.5 = (f32[128,128]{1,0:T(8,128)S(1)}, f32[128,128]{1,0:T(8,128)}, u32[]{:S(2)}) copy-start(f32[128,128]{1,0:T(8,128)} %param.12) | copy-start | bytes 196612
  0.0 10.2 %copy-start.6 = (f32[128,128]{1,0:T(8,128)S(1)}, f32[128,128]{1,0:T(8,128)}, u32[]{:S(2)}) copy-start(f32[128,128]{1,0:T(8,128)} %param.11) | copy-start | bytes 196612
  0.0 10.2 %copy-start.7 = (s32[128,128]{1,0:T(8,128)S(1)}, s32[128,128]{1,0:T(8,128)}, u32[]{:S(2)}) copy-start(s32[128,128]{1,0:T(8,128)} %param.13) | copy-start | bytes 196612
  2.8 17.3 %collective-permute-start = (f32[1,128,2048]{2,1,0:T(8,128)}, f32[1,128,2048]{2,1,0:T(8,128)S(1)}, u32[]{:S(2)}, u32[]{:S(2)}) collective-permute-start(f32[1,128,2048]{2,1,0:T(8,128)} %get-tuple-element.229), channel_id=1, source_target_pairs={{0,8},{8,16},{16,24},{24,32},{32,40},{40,48},{48,56},{56,64},{64,7... | collective-permute-start | bytes 3145736 | tf_op jit(solution)/shard_map/ppermute | solution.py:15
  8.1 17.3 %collective-permute-start.1 = (f32[1,128,2048]{2,1,0:T(8,128)S(1)}, f32[1,128,2048]{2,1,0:T(8,128)S(1)}, u32[]{:S(2)}, u32[]{:S(2)}) collective-permute-start(f32[1,128,2048]{2,1,0:T(8,128)S(1)} %get-tuple-element.230), channel_id=1, source_target_pairs={{8,0},{16,8},{24,16},{32,24},{40,32},{48,40},{56,48},{64,56},{72,6... | collective-permute-start | bytes 3145736 | tf_op jit(solution)/shard_map/ppermute | solution.py:18
  32.8 4.6 %copy-start.2 = (f32[4,128,2048]{2,1,0:T(8,128)S(1)}, f32[4,128,2048]{2,1,0:T(8,128)}, u32[]{:S(2)}) copy-start(f32[4,128,2048]{2,1,0:T(8,128)} %get-tuple-element.316) | copy-start | bytes 12582916 | tf_op jit(solution)/shard_map/while
  39.0 2.0 %copy-start.3 = (f32[4,128,2048]{2,1,0:T(8,128)}, f32[4,128,2048]{2,1,0:T(8,128)S(1)}, u32[]{:S(2)}) copy-start(f32[4,128,2048]{2,1,0:T(8,128)S(1)} %fusion.45) | copy-start | bytes 12582916 | tf_op jit(solution)/shard_map/while
  42.2 4.6 %copy-start.2 = (f32[4,128,2048]{2,1,0:T(8,128)S(1)}, f32[4,128,2048]{2,1,0:T(8,128)}, u32[]{:S(2)}) copy-start(f32[4,128,2048]{2,1,0:T(8,128)} %get-tuple-element.316) | copy-start | bytes 12582916 | tf_op jit(solution)/shard_map/while
  48.4 2.0 %copy-start.3 = (f32[4,128,2048]{2,1,0:T(8,128)}, f32[4,128,2048]{2,1,0:T(8,128)S(1)}, u32[]{:S(2)}) copy-start(f32[4,128,2048]{2,1,0:T(8,128)S(1)} %fusion.45) | copy-start | bytes 12582916 | tf_op jit(solution)/shard_map/while
  51.6 4.6 %copy-start.2 = (f32[4,128,2048]{2,1,0:T(8,128)S(1)}, f32[4,128,2048]{2,1,0:T(8,128)}, u32[]{:S(2)}) copy-start(f32[4,128,2048]{2,1,0:T(8,128)} %get-tuple-element.316) | copy-start | bytes 12582916 | tf_op jit(solution)/shard_map/while
  57.7 2.0 %copy-start.3 = (f32[4,128,2048]{2,1,0:T(8,128)}, f32[4,128,2048]{2,1,0:T(8,128)S(1)}, u32[]{:S(2)}) copy-start(f32[4,128,2048]{2,1,0:T(8,128)S(1)} %fusion.45) | copy-start | bytes 12582916 | tf_op jit(solution)/shard_map/while
  60.9 4.6 %copy-start.2 = (f32[4,128,2048]{2,1,0:T(8,128)S(1)}, f32[4,128,2048]{2,1,0:T(8,128)}, u32[]{:S(2)}) copy-start(f32[4,128,2048]{2,1,0:T(8,128)} %get-tuple-element.316) | copy-start | bytes 12582916 | tf_op jit(solution)/shard_map/while
  67.1 2.0 %copy-start.3 = (f32[4,128,2048]{2,1,0:T(8,128)}, f32[4,128,2048]{2,1,0:T(8,128)S(1)}, u32[]{:S(2)}) copy-start(f32[4,128,2048]{2,1,0:T(8,128)S(1)} %fusion.45) | copy-start | bytes 12582916 | tf_op jit(solution)/shard_map/while
  71.9 14.0 %collective-permute-start.2 = (f32[1,128,2048]{2,1,0:T(8,128)}, f32[1,128,2048]{2,1,0:T(8,128)S(1)}, u32[]{:S(2)}, u32[]{:S(2)}) collective-permute-start(f32[1,128,2048]{2,1,0:T(8,128)} %get-tuple-element.227), channel_id=1, source_target_pairs={{0,8},{8,16},{16,24},{24,32},{32,40},{40,48},{48,56},{56,64},{64,7... | collective-permute-start | bytes 3145736 | tf_op jit(solution)/shard_map/ppermute | solution.py:15
  73.8 17.3 %collective-permute-start.3 = (f32[1,128,2048]{2,1,0:T(8,128)S(1)}, f32[1,128,2048]{2,1,0:T(8,128)S(1)}, u32[]{:S(2)}, u32[]{:S(2)}) collective-permute-start(f32[1,128,2048]{2,1,0:T(8,128)S(1)} %get-tuple-element.228), channel_id=1, source_target_pairs={{8,0},{16,8},{24,16},{32,24},{40,32},{48,40},{56,48},{64,56},{72,6... | collective-permute-start | bytes 3145736 | tf_op jit(solution)/shard_map/ppermute | solution.py:18
  97.4 10.2 %collective-permute-start.4 = (f32[512,1,128]{2,1,0:T(1,128)S(1)}, f32[512,1,128]{2,1,0:T(1,128)S(1)}, u32[]{:S(2)}, u32[]{:S(2)}) collective-permute-start(f32[512,1,128]{2,1,0:T(1,128)S(1)} %get-tuple-element.225), channel_id=1, source_target_pairs={{0,1},{1,2},{2,3},{3,4},{4,5},{5,6},{6,7},{8,9},{9,10},{10,11},{11... | collective-permute-start | bytes 786440 | tf_op jit(solution)/shard_map/ppermute | solution.py:15
  101.4 11.9 %collective-permute-start.5 = (f32[512,1,128]{2,1,0:T(1,128)S(1)}, f32[512,1,128]{2,1,0:T(1,128)S(1)}, u32[]{:S(2)}, u32[]{:S(2)}) collective-permute-start(f32[512,1,128]{2,1,0:T(1,128)S(1)} %get-tuple-element.226), channel_id=1, source_target_pairs={{1,0},{2,1},{3,2},{4,3},{5,4},{6,5},{7,6},{9,8},{10,9},{11,10},{12... | collective-permute-start | bytes 786440 | tf_op jit(solution)/shard_map/ppermute | solution.py:18
  116.5 4.9 %copy-start = (f32[512,16,128]{2,1,0:T(8,128)S(1)}, f32[512,16,128]{2,1,0:T(8,128)}, u32[]{:S(2)}) copy-start(f32[512,16,128]{2,1,0:T(8,128)} %get-tuple-element.334) | copy-start | bytes 12582916 | tf_op jit(solution)/shard_map/while
  125.6 2.0 %copy-start.1 = (f32[512,16,128]{2,1,0:T(8,128)}, f32[512,16,128]{2,1,0:T(8,128)S(1)}, u32[]{:S(2)}) copy-start(f32[512,16,128]{2,1,0:T(8,128)S(1)} %fusion.48) | copy-start | bytes 12582916 | tf_op jit(solution)/shard_map/while
  127.7 4.9 %copy-start = (f32[512,16,128]{2,1,0:T(8,128)S(1)}, f32[512,16,128]{2,1,0:T(8,128)}, u32[]{:S(2)}) copy-start(f32[512,16,128]{2,1,0:T(8,128)} %get-tuple-element.334) | copy-start | bytes 12582916 | tf_op jit(solution)/shard_map/while
  136.9 2.0 %copy-start.1 = (f32[512,16,128]{2,1,0:T(8,128)}, f32[512,16,128]{2,1,0:T(8,128)S(1)}, u32[]{:S(2)}) copy-start(f32[512,16,128]{2,1,0:T(8,128)S(1)} %fusion.48) | copy-start | bytes 12582916 | tf_op jit(solution)/shard_map/while
  139.0 4.9 %copy-start = (f32[512,16,128]{2,1,0:T(8,128)S(1)}, f32[512,16,128]{2,1,0:T(8,128)}, u32[]{:S(2)}) copy-start(f32[512,16,128]{2,1,0:T(8,128)} %get-tuple-element.334) | copy-start | bytes 12582916 | tf_op jit(solution)/shard_map/while
  148.2 2.0 %copy-start.1 = (f32[512,16,128]{2,1,0:T(8,128)}, f32[512,16,128]{2,1,0:T(8,128)S(1)}, u32[]{:S(2)}) copy-start(f32[512,16,128]{2,1,0:T(8,128)S(1)} %fusion.48) | copy-start | bytes 12582916 | tf_op jit(solution)/shard_map/while
  150.3 4.9 %copy-start = (f32[512,16,128]{2,1,0:T(8,128)S(1)}, f32[512,16,128]{2,1,0:T(8,128)}, u32[]{:S(2)}) copy-start(f32[512,16,128]{2,1,0:T(8,128)} %get-tuple-element.334) | copy-start | bytes 12582916 | tf_op jit(solution)/shard_map/while
  159.5 2.0 %copy-start.1 = (f32[512,16,128]{2,1,0:T(8,128)}, f32[512,16,128]{2,1,0:T(8,128)S(1)}, u32[]{:S(2)}) copy-start(f32[512,16,128]{2,1,0:T(8,128)S(1)} %fusion.48) | copy-start | bytes 12582916 | tf_op jit(solution)/shard_map/while
  164.1 11.2 %collective-permute-start.6 = (f32[512,1,128]{2,1,0:T(1,128)S(1)}, f32[512,1,128]{2,1,0:T(1,128)S(1)}, u32[]{:S(2)}, u32[]{:S(2)}) collective-permute-start(f32[512,1,128]{2,1,0:T(1,128)S(1)} %get-tuple-element.223), channel_id=1, source_target_pairs={{0,1},{1,2},{2,3},{3,4},{4,5},{5,6},{6,7},{8,9},{9,10},{10,11},{11... | collective-permute-start | bytes 786440 | tf_op jit(solution)/shard_map/ppermute | solution.py:15
  168.1 13.8 %collective-permute-start.7 = (f32[512,1,128]{2,1,0:T(1,128)S(1)}, f32[512,1,128]{2,1,0:T(1,128)S(1)}, u32[]{:S(2)}, u32[]{:S(2)}) collective-permute-start(f32[512,1,128]{2,1,0:T(1,128)S(1)} %get-tuple-element.224), channel_id=1, source_target_pairs={{1,0},{2,1},{3,2},{4,3},{5,4},{6,5},{7,6},{9,8},{10,9},{11,10},{12... | collective-permute-start | bytes 786440 | tf_op jit(solution)/shard_map/ppermute | solution.py:18
where the time goes:
time: 193 us; the launch traced here: 192 us
  local copies, waits for them, and re-layouts  77.6 us (40%)
  waiting for transfers between devices  49.9 us (26%)
  other arithmetic  39.1 us (20%)
  starting transfers between devices  25.3 us (13%)
    slice x16, local copies, waits for them, and re-layouts, subcycle(): east_cell = jnp.roll(current, -1, axis=lon_axis)  47.6 us
    ppermute x4, waiting for transfers between devices, extended(): lax.ppermute(lax.slice_in_dim(block, block.shape[dim] - width, None, axis...  26.9 us
    ppermute x4, waiting for transfers between devices, extended(): lax.ppermute(lax.slice_in_dim(block, 0, width, axis=dim), axis, backward)  23 us
    sub x4, other arithmetic, lat_update(): return center - courant * (center - nearby)  20.8 us
    sub x8, other arithmetic, subcycle(): return current - cell_rate * (current - nearby)  17.6 us
    while x32, local copies, waits for them, and re-layouts  16.4 us
    ppermute x4, starting transfers between devices, extended(): lax.ppermute(lax.slice_in_dim(block, block.shape[dim] - width, None, axis...  15.3 us
    ppermute x4, starting transfers between devices, extended(): lax.ppermute(lax.slice_in_dim(block, 0, width, axis=dim), axis, backward)  10 us
  transfers between devices with their start and end apart: 8, of which 8 were waited for; matrix products, arithmetic and copies ran while one was open for 0% of the time, Pallas kernels for 0%

commit v1 on v0

v1 whole, which is shorter than its diff:
```python
import functools

import jax
import jax.numpy as jnp
from jax import lax
from jax.experimental import pallas as pl
from jax.experimental.pallas import tpu as pltpu
from jax.sharding import PartitionSpec as P

MESH = pl.DeviceIdType.MESH
NLAT = 128
NLON = 128
SUBCYCLES = 4
WIDE = 256
F32 = jnp.float32
BF16 = jnp.bfloat16


def split(values):
    high = values.astype(BF16)
    return high, (values - high.astype(F32)).astype(BF16)


def dot(a, b):
    return jnp.dot(a, b, preferred_element_type=F32)


def upwind(center, below, above, courant, from_below):
    nearby = jnp.where(from_below, below, above)
    return center - courant * (center - nearby)


def sweep_matrix(lat, lon_ref, zonal_ref, counts_ref):
    rate = lon_ref[pl.ds(lat, 1), :]
    west = jnp.broadcast_to(zonal_ref[pl.ds(lat, 1), :], (NLON, NLON)) == 1
    count = counts_ref[lat]
    row = lax.broadcasted_iota(jnp.int32, (NLON, NLON), 0)
    column = lax.broadcasted_iota(jnp.int32, (NLON, NLON), 1)
    current = jnp.where(row == column, 1.0, 0.0).astype(F32)
    for cycle in range(SUBCYCLES):
        cell_rate = jnp.where(cycle < count, rate, 0.0)
        nearby = jnp.where(
            west, pltpu.roll(current, 1, 1), pltpu.roll(current, NLON - 1, 1)
        )
        current = current - cell_rate * (current - nearby)
    return current


def kernel(
    rows_n, cols_n,
    cov, lon_ref, lat_ref, zonal_ref, sign_ref, counts_ref,
    out,
    ext, wide, row_mid, col_mid, final,
    row_rate, row_sign, row_hi, row_lo, col_hi, col_lo,
    load_sem, row_send, row_recv, col_send, col_recv, out_sem,
):
    r, c = lax.axis_index("row"), lax.axis_index("col")
    rows, cols = cov.shape
    row_lats, col_lats = rows // NLON, cols // NLON
    chunks = cols // WIDE
    halo = 2 * NLON
    first_row, first_col = r * row_lats, c * col_lats
    has_down, has_up = r > 0, r < rows_n - 1
    has_left, has_right = c > 0, c < cols_n - 1
    down, up = (r - 1, c), (r + 1, c)
    left, right = (r, c - 1), (r, c + 1)

    barrier = pltpu.get_barrier_semaphore()
    for exists, device in ((has_down, down), (has_up, up), (has_left, left), (has_right, right)):
        @pl.when(exists)
        def _():
            pl.semaphore_signal(barrier, inc=1, device_id=device, device_id_type=MESH)

    load = pltpu.make_async_copy(cov, ext.at[pl.ds(halo, rows), :], load_sem)
    load.start()

    pl.semaphore_wait(
        barrier,
        has_down.astype(jnp.int32) + has_up.astype(jnp.int32)
        + has_left.astype(jnp.int32) + has_right.astype(jnp.int32),
    )

    def chunk_columns(chunk):
        return pl.ds(pl.multiple_of(chunk * WIDE, WIDE), WIDE)

    def to_down(chunk):
        return pltpu.make_async_remote_copy(
            cov.at[pl.ds(0, halo), chunk_columns(chunk)],
            ext.at[pl.ds(halo + rows, halo), chunk_columns(chunk)],
            row_send.at[0, chunk], row_recv.at[0, chunk],
            device_id=down, device_id_type=MESH,
        )

    def to_up(chunk):
        return pltpu.make_async_remote_copy(
            cov.at[pl.ds(rows - halo, halo), chunk_columns(chunk)],
            ext.at[pl.ds(0, halo), chunk_columns(chunk)],
            row_send.at[1, chunk], row_recv.at[1, chunk],
            device_id=up, device_id_type=MESH,
        )

    order = [0, chunks - 1, *range(1, chunks - 1)]

    @pl.when(has_down)
    def _():
        for chunk in order:
            to_down(chunk).start()

    @pl.when(has_up)
    def _():
        for chunk in order:
            to_up(chunk).start()

    @pl.when(jnp.logical_not(has_down))
    def _():
        ext[pl.ds(0, halo), :] = jnp.zeros((halo, cols), F32)

    @pl.when(jnp.logical_not(has_up))
    def _():
        ext[pl.ds(halo + rows, halo), :] = jnp.zeros((halo, cols), F32)

    @pl.when(jnp.logical_not(has_left))
    def _():
        wide[:, pl.ds(0, halo)] = jnp.zeros((rows, halo), F32)

    @pl.when(jnp.logical_not(has_right))
    def _():
        wide[:, pl.ds(halo + cols, halo)] = jnp.zeros((rows, halo), F32)

    def clamped(lat):
        return jnp.clip(lat, 0, NLAT - 1)

    def courant_of(lat):
        inside = jnp.logical_and(lat >= 0, lat < NLAT)
        return jnp.where(inside, lat_ref[pl.ds(clamped(lat), 1), :], 0.0)

    def prepare_row(i, carry):
        lat = first_row - 1 + i
        at = clamped(lat)
        row_rate[i] = jnp.broadcast_to(courant_of(lat), (NLON, NLON)).T
        row_sign[i] = jnp.broadcast_to(
            sign_ref[pl.ds(at, 1), :].astype(F32), (NLON, NLON)
        ).T
        high, low = split(sweep_matrix(at, lon_ref, zonal_ref, counts_ref).T)
        row_hi[i] = high
        row_lo[i] = low
        return carry

    lax.fori_loop(0, row_lats + 2, prepare_row, 0)

    def prepare_col(i, carry):
        at = clamped(first_col - 1 + i)
        high, low = split(sweep_matrix(at, lon_ref, zonal_ref, counts_ref))
        col_hi[i] = high
        col_lo[i] = low
        return carry

    def both(table):
        return jnp.concatenate([table, table], axis=1)

    def row_chunk(chunk):
        @pl.when(has_down)
        def _():
            to_up(chunk).wait_recv()

        @pl.when(has_up)
        def _():
            to_down(chunk).wait_recv()

        at = chunk_columns(chunk)
        for i in range(row_lats + 2):
            below = ext[pl.ds(i * NLON, NLON), at]
            center = ext[pl.ds((i + 1) * NLON, NLON), at]
            above = ext[pl.ds((i + 2) * NLON, NLON), at]
            moved = upwind(center, below, above, both(row_rate[i]), both(row_sign[i]) == 1.0)
            high, low = split(moved)
            row_mid[i] = (
                dot(row_hi[i], high) + (dot(row_hi[i], low) + dot(row_lo[i], high))
            )
        own = pl.ds(pl.multiple_of(halo + chunk * WIDE, WIDE), WIDE)
        for i in range(1, row_lats + 1):
            wide[pl.ds((i - 1) * NLON, NLON), own] = upwind(
                row_mid[i], row_mid[i - 1], row_mid[i + 1],
                both(row_rate[i]), both(row_sign[i]) == 1.0,
            )

    def lat_columns(index):
        return pl.ds(pl.multiple_of(index * NLON, NLON), NLON)

    def col_middle(i):
        lat = first_col - 1 + i
        from_below = sign_ref[pl.ds(clamped(lat), 1), :] == 1
        moved = upwind(
            wide[:, lat_columns(i + 1)], wide[:, lat_columns(i)], wide[:, lat_columns(i + 2)],
            courant_of(lat), from_below,
        )
        high, low = split(moved)
        col_mid[:, lat_columns(i)] = (
            dot(high, col_hi[i]) + (dot(low, col_hi[i]) + dot(high, col_lo[i]))
        )

    def col_final(k):
        lat = first_col + k
        from_below = sign_ref[pl.ds(lat, 1), :] == 1
        final[:, lat_columns(k)] = upwind(
            col_mid[:, lat_columns(k + 1)], col_mid[:, lat_columns(k)],
            col_mid[:, lat_columns(k + 2)], courant_of(lat), from_below,
        )

    def to_left():
        return pltpu.make_async_remote_copy(
            wide.at[:, pl.ds(halo, halo)], wide.at[:, pl.ds(halo + cols, halo)],
            col_send.at[0], col_recv.at[0], device_id=left, device_id_type=MESH,
        )

    def to_right():
        return pltpu.make_async_remote_copy(
            wide.at[:, pl.ds(cols, halo)], wide.at[:, pl.ds(0, halo)],
            col_send.at[1], col_recv.at[1], device_id=right, device_id_type=MESH,
        )

    load.wait()
    row_chunk(0)

    @pl.when(has_left)
    def _():
        to_left().start()

    row_chunk(chunks - 1)

    @pl.when(has_right)
    def _():
        to_right().start()

    lax.fori_loop(0, col_lats + 2, prepare_col, 0)

    def interior(chunk, carry):
        row_chunk(chunk)
        return carry

    lax.fori_loop(1, chunks - 1, interior, 0)

    def middle(i, carry):
        col_middle(i)
        return carry

    def finish(k, carry):
        col_final(k)
        return carry

    lax.fori_loop(2, col_lats, middle, 0)
    lax.fori_loop(2, col_lats - 2, finish, 0)
    inner = pl.ds(halo, cols - 2 * halo)
    store_inner = pltpu.make_async_copy(final.at[:, inner], out.at[:, inner], out_sem.at[0])
    store_inner.start()

    @pl.when(has_right)
    def _():
        to_left().wait_recv()

    col_middle(col_lats)
    col_middle(col_lats + 1)
    col_final(col_lats - 2)
    col_final(col_lats - 1)
    high_edge = pl.ds(cols - halo, halo)
    store_high = pltpu.make_async_copy(final.at[:, high_edge], out.at[:, high_edge], out_sem.at[1])
    store_high.start()

    @pl.when(has_left)
    def _():
        to_right().wait_recv()

    col_middle(0)
    col_middle(1)
    col_final(0)
    col_final(1)
    low_edge = pl.ds(0, halo)
    store_low = pltpu.make_async_copy(final.at[:, low_edge], out.at[:, low_edge], out_sem.at[2])
    store_low.start()

    @pl.when(has_down)
    def _():
        for chunk in order:
            to_down(chunk).wait_send()

    @pl.when(has_up)
    def _():
        for chunk in order:
            to_up(chunk).wait_send()

    @pl.when(has_left)
    def _():
        to_left().wait_send()

    @pl.when(has_right)
    def _():
        to_right().wait_send()

    store_inner.wait()
    store_high.wait()
    store_low.wait()


def solution(mesh):
    rows_n, cols_n = mesh.shape["row"], mesh.shape["col"]

    def per_device(covariance, lon_courant, lat_courant, zonal_upwind_sign, lat_sign, cycle_counts):
        rows, cols = covariance.shape
        row_lats, col_lats = rows // NLON, cols // NLON
        chunks = cols // WIDE
        vmem = pl.BlockSpec(memory_space=pltpu.VMEM)
        return pl.pallas_call(
            functools.partial(kernel, rows_n, cols_n),
            out_shape=jax.ShapeDtypeStruct((rows, cols), F32),
            in_specs=[
                pl.BlockSpec(memory_space=pl.ANY), vmem, vmem, vmem, vmem,
                pl.BlockSpec(memory_space=pltpu.SMEM),
            ],
            out_specs=pl.BlockSpec(memory_space=pl.ANY),
            scratch_shapes=[
                pltpu.VMEM((rows + 4 * NLON, cols), F32),
                pltpu.VMEM((rows, cols + 4 * NLON), F32),
                pltpu.VMEM((row_lats + 2, NLON, WIDE), F32),
                pltpu.VMEM((rows, cols + 2 * NLON), F32),
                pltpu.VMEM((rows, cols), F32),
                pltpu.VMEM((row_lats + 2, NLON, NLON), F32),
                pltpu.VMEM((row_lats + 2, NLON, NLON), F32),
                pltpu.VMEM((row_lats + 2, NLON, NLON), BF16),
                pltpu.VMEM((row_lats + 2, NLON, NLON), BF16),
                pltpu.VMEM((col_lats + 2, NLON, NLON), BF16),
                pltpu.VMEM((col_lats + 2, NLON, NLON), BF16),
                pltpu.SemaphoreType.DMA,
                pltpu.SemaphoreType.DMA((2, chunks)),
                pltpu.SemaphoreType.DMA((2, chunks)),
                pltpu.SemaphoreType.DMA((2,)),
                pltpu.SemaphoreType.DMA((2,)),
                pltpu.SemaphoreType.DMA((3,)),
            ],
            name="forecast",
            compiler_params=pltpu.CompilerParams(
                collective_id=0, has_side_effects=True, vmem_limit_bytes=40 * 2**20
            ),
        )(covariance, lon_courant, lat_courant, zonal_upwind_sign, lat_sign, cycle_counts)

    placed = (P("row", "col"), P(), P(), P(), P(), P())
    return jax.shard_map(
        per_device, mesh=mesh, in_specs=placed, out_specs=P("row", "col"), check_vma=False
    )
```

time: 193 us -> 64.8 us (0.34)
  the two profiles are of different devices: /device:TPU:103 before, /device:TPU:9 now
where the time goes in v1:
time: 64.8 us; the launch traced here: 64.5 us
  Pallas kernels  56.3 us (87%)
  local copies, waits for them, and re-layouts  8.21 us (13%)
    pallas_call x1, Pallas kernels, per_device(): pl.pallas_call(functools.partial(kernel, rows_n, cols_n), out_shape=jax.S...  56.3 us
    unnamed x13, local copies, waits for them, and re-layouts  8.21 us

profile of v1, /device:TPU:9, one launch (start us, length us, event | category | flops | bytes accessed | tf_op | source)
XLA Modules:
  0.0 64.5 jit_solution(11214686051561005190)
XLA Ops:
  0.0 0.0 copy-start
  0.0 2.2 %copy-done = f32[512,2048]{1,0:T(8,128)S(1)} copy-done((f32[512,2048]{1,0:T(8,128)S(1)}, f32[512,2048]{1,0:T(8,128)}, u32[]{:S(2)}) %copy-start) | copy-done | bytes 4194328
  2.2 0.0 copy-start.1
  2.2 0.8 %copy-done.1 = f32[128,128]{1,0:T(8,128)S(1)} copy-done((f32[128,128]{1,0:T(8,128)S(1)}, f32[128,128]{1,0:T(8,128)}, u32[]{:S(2)}) %copy-start.1) | copy-done | bytes 65560
  3.0 0.0 copy-start.2
  3.0 0.8 %copy-done.2 = f32[128,128]{1,0:T(8,128)S(1)} copy-done((f32[128,128]{1,0:T(8,128)S(1)}, f32[128,128]{1,0:T(8,128)}, u32[]{:S(2)}) %copy-start.2) | copy-done | bytes 65560
  3.9 0.0 copy-start.3
  3.9 0.8 %copy-done.3 = s32[128,128]{1,0:T(8,128)S(1)} copy-done((s32[128,128]{1,0:T(8,128)S(1)}, s32[128,128]{1,0:T(8,128)}, u32[]{:S(2)}) %copy-start.3) | copy-done | bytes 65560
  4.7 0.0 copy-start.4
  4.7 0.8 %copy-done.4 = s32[128,128]{1,0:T(8,128)S(1)} copy-done((s32[128,128]{1,0:T(8,128)S(1)}, s32[128,128]{1,0:T(8,128)}, u32[]{:S(2)}) %copy-start.4) | copy-done | bytes 65560
  5.5 0.0 copy-start.5
  5.6 0.7 %copy-done.5 = s32[128]{0:T(128)S(1)} copy-done((s32[128]{0:T(128)S(1)}, s32[128]{0:T(128)}, u32[]{:S(2)}) %copy-start.5) | copy-done | bytes 536
  6.2 56.3 %forecast.1 = f32[512,2048]{1,0:T(8,128)S(1)} custom-call(f32[512,2048]{1,0:T(8,128)S(1)} %copy-done, f32[128,128]{1,0:T(8,128)S(1)} %copy-done.1, f32[128,128]{1,0:T(8,128)S(1)} %copy-done.2, s32[128,128]{1,0:T(8,128)S(1)} %copy-done.3, s32[128,128]{1,0:T(8,128)S(1)} %copy-done.4, s32[128]{0:T(128)S(1)} %copy-done.5), custom_call_target="tpu_custom_call" | custom-call | tf_op jit(solution)/shard_map/forecast/pallas_call | solution.py:312
  62.5 2.0 %copy.8 = f32[512,2048]{1,0:T(8,128)} copy(f32[512,2048]{1,0:T(8,128)S(1)} %forecast.1) | data formatting | bytes 8388608
Async XLA Ops:
  0.0 2.2 %copy-start = (f32[512,2048]{1,0:T(8,128)S(1)}, f32[512,2048]{1,0:T(8,128)}, u32[]{:S(2)}) copy-start(f32[512,2048]{1,0:T(8,128)} %cov.1) | copy-start | bytes 12582916
  2.2 0.8 %copy-start.1 = (f32[128,128]{1,0:T(8,128)S(1)}, f32[128,128]{1,0:T(8,128)}, u32[]{:S(2)}) copy-start(f32[128,128]{1,0:T(8,128)} %lon_ref.1) | copy-start | bytes 196612
  3.0 0.8 %copy-start.2 = (f32[128,128]{1,0:T(8,128)S(1)}, f32[128,128]{1,0:T(8,128)}, u32[]{:S(2)}) copy-start(f32[128,128]{1,0:T(8,128)} %lat_ref.1) | copy-start | bytes 196612
  3.9 0.8 %copy-start.3 = (s32[128,128]{1,0:T(8,128)S(1)}, s32[128,128]{1,0:T(8,128)}, u32[]{:S(2)}) copy-start(s32[128,128]{1,0:T(8,128)} %zonal_ref.1) | copy-start | bytes 196612
  4.7 0.8 %copy-start.4 = (s32[128,128]{1,0:T(8,128)S(1)}, s32[128,128]{1,0:T(8,128)}, u32[]{:S(2)}) copy-start(s32[128,128]{1,0:T(8,128)} %sign_ref.1) | copy-start | bytes 196612
  5.5 0.7 %copy-start.5 = (s32[128]{0:T(128)S(1)}, s32[128]{0:T(128)}, u32[]{:S(2)}) copy-start(s32[128]{0:T(128)} %counts_ref.1) | copy-start | bytes 1540

commit v2 on v1

v2 whole, which is shorter than its diff:
```python
import functools

import jax
import jax.numpy as jnp
from jax import lax
from jax.experimental import pallas as pl
from jax.experimental.pallas import tpu as pltpu
from jax.sharding import PartitionSpec as P

MESH = pl.DeviceIdType.MESH
NLAT = 128
NLON = 128
SUBCYCLES = 4
WIDE = 256
RELAYED = (5, 6, 8, 9)
F32 = jnp.float32
BF16 = jnp.bfloat16


def split(values):
    high = values.astype(BF16)
    return high, (values - high.astype(F32)).astype(BF16)


def dot(a, b):
    return jnp.dot(a, b, preferred_element_type=F32)


def upwind(center, below, above, courant, from_below):
    nearby = jnp.where(from_below, below, above)
    return center - courant * (center - nearby)


def sweep_matrix(lat, lon_ref, zonal_ref, counts_ref):
    rate = lon_ref[pl.ds(lat, 1), :]
    west = jnp.broadcast_to(zonal_ref[pl.ds(lat, 1), :], (NLON, NLON)) == 1
    count = counts_ref[lat]
    row = lax.broadcasted_iota(jnp.int32, (NLON, NLON), 0)
    column = lax.broadcasted_iota(jnp.int32, (NLON, NLON), 1)
    current = jnp.where(row == column, 1.0, 0.0).astype(F32)
    for cycle in range(SUBCYCLES):
        cell_rate = jnp.where(cycle < count, rate, 0.0)
        nearby = jnp.where(
            west, pltpu.roll(current, 1, 1), pltpu.roll(current, NLON - 1, 1)
        )
        current = current - cell_rate * (current - nearby)
    return current


def kernel(
    rows_n, cols_n,
    cov, lon_hbm, lat_hbm, zonal_hbm, sign_hbm, counts_hbm,
    final,
    ext, wide, relayed, row_mid, col_mid,
    lon_ref, lat_ref, zonal_ref, sign_ref, counts_ref,
    row_rate, row_sign, row_hi, row_lo, col_hi, col_lo,
    load_sem, table_sem, row_send, row_recv, relay_recv, relay_send, col_send, col_recv,
):
    r, c = lax.axis_index("row"), lax.axis_index("col")
    rows, cols = cov.shape
    row_lats, col_lats = rows // NLON, cols // NLON
    halo = 2 * NLON
    inner = cols // WIDE - 2
    first_row, first_col = r * row_lats, c * col_lats
    has_down, has_up = r > 0, r < rows_n - 1
    has_left, has_right = c > 0, c < cols_n - 1
    down, up = (r - 1, c), (r + 1, c)
    left, right = (r, c - 1), (r, c + 1)

    half = rows_n // 2
    below_gap, above_gap = r == half - 1, r == half
    bottom, top = r == 0, r == rows_n - 1
    via_top = (rows_n - 1, c)
    via_bottom = (0, c)
    to_below_gap, to_above_gap = (half - 1, c), (half, c)

    barrier = pltpu.get_barrier_semaphore()
    links = (
        (has_down, down), (has_up, up), (has_left, left), (has_right, right),
        (below_gap, via_top), (top, to_below_gap), (top, to_above_gap), (above_gap, via_top),
        (above_gap, via_bottom), (bottom, to_above_gap), (bottom, to_below_gap), (below_gap, via_bottom),
    )
    for exists, device in links:
        @pl.when(exists)
        def _():
            pl.semaphore_signal(barrier, inc=1, device_id=device, device_id_type=MESH)

    tables = [
        pltpu.make_async_copy(source, target, table_sem.at[i])
        for i, (source, target) in enumerate((
            (lat_hbm, lat_ref), (sign_hbm, sign_ref), (lon_hbm, lon_ref),
            (zonal_hbm, zonal_ref), (counts_hbm, counts_ref),
        ))
    ]
    for table in tables:
        table.start()
    load = pltpu.make_async_copy(cov, ext.at[pl.ds(halo, rows), :], load_sem)
    load.start()

    pl.semaphore_wait(barrier, sum(exists.astype(jnp.int32) for exists, _ in links))

    def piece_columns(piece):
        if piece < 4:
            lat = (0, 1, col_lats - 2, col_lats - 1)[piece]
            return pl.ds(lat * NLON, NLON)
        return inner_columns(piece - 4)

    def inner_columns(chunk):
        return pl.ds(pl.multiple_of((chunk + 1) * WIDE, WIDE), WIDE)

    def to_down(piece, at):
        return pltpu.make_async_remote_copy(
            cov.at[pl.ds(0, halo), at], ext.at[pl.ds(halo + rows, halo), at],
            row_send.at[0, piece], row_recv.at[0, piece],
            device_id=down, device_id_type=MESH,
        )

    def to_up(piece, at):
        return pltpu.make_async_remote_copy(
            cov.at[pl.ds(rows - halo, halo), at], ext.at[pl.ds(0, halo), at],
            row_send.at[1, piece], row_recv.at[1, piece],
            device_id=up, device_id_type=MESH,
        )

    def to_relay(piece, at, rising):
        return pltpu.make_async_remote_copy(
            cov.at[pl.ds(rows - halo if rising else 0, halo), at], relayed.at[:, at],
            row_send.at[int(rising), piece], relay_recv.at[piece],
            device_id=via_top if rising else via_bottom, device_id_type=MESH,
        )

    def from_relay(piece, at, rising):
        return pltpu.make_async_remote_copy(
            relayed.at[:, at], ext.at[pl.ds(0 if rising else halo + rows, halo), at],
            relay_send.at[piece], row_recv.at[int(rising), piece],
            device_id=to_above_gap if rising else to_below_gap, device_id_type=MESH,
        )

    order = (0, 3, 1, 2, *range(4, 4 + inner))
    for piece in order:
        at = piece_columns(piece)
        if piece in RELAYED:
            @pl.when(above_gap)
            def _():
                to_relay(piece, at, False).start()

            @pl.when(below_gap)
            def _():
                to_relay(piece, at, True).start()

            @pl.when(jnp.logical_and(has_down, jnp.logical_not(above_gap)))
            def _():
                to_down(piece, at).start()

            @pl.when(jnp.logical_and(has_up, jnp.logical_not(below_gap)))
            def _():
                to_up(piece, at).start()
        else:
            @pl.when(has_down)
            def _():
                to_down(piece, at).start()

            @pl.when(has_up)
            def _():
                to_up(piece, at).start()

    @pl.when(jnp.logical_not(has_down))
    def _():
        ext[pl.ds(0, halo), :] = jnp.zeros((halo, cols), F32)

    @pl.when(jnp.logical_not(has_up))
    def _():
        ext[pl.ds(halo + rows, halo), :] = jnp.zeros((halo, cols), F32)

    @pl.when(jnp.logical_not(has_left))
    def _():
        wide[:, pl.ds(0, halo)] = jnp.zeros((rows, halo), F32)

    @pl.when(jnp.logical_not(has_right))
    def _():
        wide[:, pl.ds(halo + cols, halo)] = jnp.zeros((rows, halo), F32)

    def clamped(lat):
        return jnp.clip(lat, 0, NLAT - 1)

    def courant_of(lat):
        inside = jnp.logical_and(lat >= 0, lat < NLAT)
        return jnp.where(inside, lat_ref[pl.ds(clamped(lat), 1), :], 0.0)

    for table in tables:
        table.wait()

    def prepare_row(i, carry):
        lat = first_row - 1 + i
        at = clamped(lat)
        row_rate[i] = jnp.broadcast_to(courant_of(lat), (NLON, NLON)).T
        row_sign[i] = jnp.broadcast_to(
            sign_ref[pl.ds(at, 1), :].astype(F32), (NLON, NLON)
        ).T
        high, low = split(sweep_matrix(at, lon_ref, zonal_ref, counts_ref).T)
        row_hi[i] = high
        row_lo[i] = low
        return carry

    lax.fori_loop(0, row_lats + 2, prepare_row, 0)

    def prepare_col(i, carry):
        at = clamped(first_col - 1 + i)
        high, low = split(sweep_matrix(at, lon_ref, zonal_ref, counts_ref))
        col_hi[i] = high
        col_lo[i] = low
        return carry

    def row_chunk(piece, start, width):
        at = pl.ds(start, width)

        @pl.when(has_down)
        def _():
            to_up(piece, at).wait_recv()

        @pl.when(has_up)
        def _():
            to_down(piece, at).wait_recv()

        def across(table):
            return jnp.concatenate([table] * (width // NLON), axis=1)

        for i in range(row_lats + 2):
            below = ext[pl.ds(i * NLON, NLON), at]
            center = ext[pl.ds((i + 1) * NLON, NLON), at]
            above = ext[pl.ds((i + 2) * NLON, NLON), at]
            moved = upwind(center, below, above, across(row_rate[i]), across(row_sign[i]) == 1.0)
            high, low = split(moved)
            row_mid[i, :, pl.ds(0, width)] = (
                dot(row_hi[i], high) + (dot(row_hi[i], low) + dot(row_lo[i], high))
            )
        mids = [row_mid[i, :, pl.ds(0, width)] for i in range(row_lats + 2)]
        own = pl.ds(pl.multiple_of(halo + start, NLON), width)
        for i in range(1, row_lats + 1):
            wide[pl.ds((i - 1) * NLON, NLON), own] = upwind(
                mids[i], mids[i - 1], mids[i + 1],
                across(row_rate[i]), across(row_sign[i]) == 1.0,
            )

    def lat_columns(index):
        return pl.ds(pl.multiple_of(index * NLON, NLON), NLON)

    def col_middle(i):
        lat = first_col - 1 + i
        from_below = sign_ref[pl.ds(clamped(lat), 1), :] == 1
        moved = upwind(
            wide[:, lat_columns(i + 1)], wide[:, lat_columns(i)], wide[:, lat_columns(i + 2)],
            courant_of(lat), from_below,
        )
        high, low = split(moved)
        col_mid[:, lat_columns(i)] = (
            dot(high, col_hi[i]) + (dot(low, col_hi[i]) + dot(high, col_lo[i]))
        )

    def col_final(k):
        lat = first_col + k
        from_below = sign_ref[pl.ds(lat, 1), :] == 1
        final[:, lat_columns(k)] = upwind(
            col_mid[:, lat_columns(k + 1)], col_mid[:, lat_columns(k)],
            col_mid[:, lat_columns(k + 2)], courant_of(lat), from_below,
        )

    def to_left(lat):
        return pltpu.make_async_remote_copy(
            wide.at[:, pl.ds(halo + lat * NLON, NLON)],
            wide.at[:, pl.ds(halo + cols + lat * NLON, NLON)],
            col_send.at[0, lat], col_recv.at[0, lat], device_id=left, device_id_type=MESH,
        )

    def to_right(lat):
        return pltpu.make_async_remote_copy(
            wide.at[:, pl.ds(cols + lat * NLON, NLON)],
            wide.at[:, pl.ds(lat * NLON, NLON)],
            col_send.at[1, lat], col_recv.at[1, lat], device_id=right, device_id_type=MESH,
        )

    def pass_on(piece, at):
        @pl.when(top)
        def _():
            to_relay(piece, at, True).wait_recv()
            from_relay(piece, at, True).start()

        @pl.when(bottom)
        def _():
            to_relay(piece, at, False).wait_recv()
            from_relay(piece, at, False).start()

    load.wait()
    for piece in (0, 3, 1, 2):
        lat = (0, 1, col_lats - 2, col_lats - 1)[piece]
        row_chunk(piece, lat * NLON, NLON)
        if piece < 2:
            @pl.when(has_left)
            def _():
                to_left(piece).start()
        else:
            @pl.when(has_right)
            def _():
                to_right(piece - 2).start()

    lax.fori_loop(0, col_lats + 2, prepare_col, 0)

    def interior(chunk, carry):
        goes_on = functools.reduce(jnp.logical_or, [chunk == piece - 4 for piece in RELAYED])

        @pl.when(goes_on)
        def _():
            pass_on(4 + chunk, inner_columns(chunk))

        row_chunk(4 + chunk, pl.multiple_of((chunk + 1) * WIDE, WIDE), WIDE)
        col_middle(2 * chunk + 2)
        col_middle(2 * chunk + 3)

        @pl.when(chunk > 0)
        def _():
            col_final(2 * chunk)
            col_final(2 * chunk + 1)

        return carry

    lax.fori_loop(0, inner, interior, 0)
    col_middle(2 * inner + 2)
    col_middle(2 * inner + 3)
    for k in range(2 * inner, 2 * inner + 2):
        col_final(k)

    @pl.when(has_right)
    def _():
        to_left(0).wait_recv()
        to_left(1).wait_recv()

    col_middle(col_lats)
    col_middle(col_lats + 1)
    col_final(col_lats - 2)
    col_final(col_lats - 1)

    @pl.when(has_left)
    def _():
        to_right(0).wait_recv()
        to_right(1).wait_recv()

    col_middle(0)
    col_middle(1)
    col_final(0)
    col_final(1)

    for piece in order:
        at = piece_columns(piece)

        @pl.when(has_down)
        def _():
            to_down(piece, at).wait_send()

        @pl.when(has_up)
        def _():
            to_up(piece, at).wait_send()

        if piece in RELAYED:
            @pl.when(jnp.logical_or(top, bottom))
            def _():
                from_relay(piece, at, True).wait_send()

    for lat in range(2):
        @pl.when(has_left)
        def _():
            to_left(lat).wait_send()

        @pl.when(has_right)
        def _():
            to_right(lat).wait_send()


def solution(mesh):
    rows_n, cols_n = mesh.shape["row"], mesh.shape["col"]

    def per_device(covariance, lon_courant, lat_courant, zonal_upwind_sign, lat_sign, cycle_counts):
        rows, cols = covariance.shape
        row_lats, col_lats = rows // NLON, cols // NLON
        pieces = cols // WIDE + 2
        hbm = pl.BlockSpec(memory_space=pltpu.HBM)
        return pl.pallas_call(
            functools.partial(kernel, rows_n, cols_n),
            out_shape=jax.ShapeDtypeStruct((rows, cols), F32),
            in_specs=[hbm] * 6,
            out_specs=pl.BlockSpec(memory_space=pltpu.VMEM),
            scratch_shapes=[
                pltpu.VMEM((rows + 4 * NLON, cols), F32),
                pltpu.VMEM((rows, cols + 4 * NLON), F32),
                pltpu.VMEM((2 * NLON, cols), F32),
                pltpu.VMEM((row_lats + 2, NLON, WIDE), F32),
                pltpu.VMEM((rows, cols + 2 * NLON), F32),
                pltpu.VMEM((NLAT, NLON), F32),
                pltpu.VMEM((NLAT, NLON), F32),
                pltpu.VMEM((NLAT, NLON), jnp.int32),
                pltpu.VMEM((NLAT, NLON), jnp.int32),
                pltpu.SMEM((NLAT,), jnp.int32),
                pltpu.VMEM((row_lats + 2, NLON, NLON), F32),
                pltpu.VMEM((row_lats + 2, NLON, NLON), F32),
                pltpu.VMEM((row_lats + 2, NLON, NLON), BF16),
                pltpu.VMEM((row_lats + 2, NLON, NLON), BF16),
                pltpu.VMEM((col_lats + 2, NLON, NLON), BF16),
                pltpu.VMEM((col_lats + 2, NLON, NLON), BF16),
                pltpu.SemaphoreType.DMA,
                pltpu.SemaphoreType.DMA((5,)),
                pltpu.SemaphoreType.DMA((2, pieces)),
                pltpu.SemaphoreType.DMA((2, pieces)),
                pltpu.SemaphoreType.DMA((pieces,)),
                pltpu.SemaphoreType.DMA((pieces,)),
                pltpu.SemaphoreType.DMA((2, 2)),
                pltpu.SemaphoreType.DMA((2, 2)),
            ],
            name="forecast",
            compiler_params=pltpu.CompilerParams(
                collective_id=0, has_side_effects=True, vmem_limit_bytes=48 * 2**20
            ),
        )(*[pltpu.with_memory_space_constraint(a, pltpu.HBM) for a in (covariance, lon_courant, lat_courant, zonal_upwind_sign, lat_sign, cycle_counts)])

    placed = (P("row", "col"), P(), P(), P(), P(), P())
    return jax.shard_map(
        per_device, mesh=mesh, in_specs=placed, out_specs=P("row", "col"), check_vma=False
    )
```

time: 64.8 us -> 47.4 us (0.73)
  Pallas kernels: 56.3 us -> 45.3 us
  local copies, waits for them, and re-layouts: 8.21 us -> 2.02 us
    pallas_call x1, Pallas kernels: 56.3 us -> 45.3 us  [per_device(): pl.pallas_call(functools.partial(kernel, rows_n, cols_n), out_shape=jax.S...]
    unnamed x13 -> x1, local copies, waits for them, and re-layouts: 8.21 us -> 2.02 us
where the time goes in v2:
time: 47.4 us; the launch traced here: 47.3 us
  Pallas kernels  45.3 us (96%)
  local copies, waits for them, and re-layouts  2.02 us (4%)
    pallas_call x1, Pallas kernels, per_device(): pl.pallas_call(functools.partial(kernel, rows_n, cols_n), out_shape=jax.S...  45.3 us
    unnamed x1, local copies, waits for them, and re-layouts  2.02 us

profile of v2, /device:TPU:9, one launch (start us, length us, event | category | flops | bytes accessed | tf_op | source)
XLA Modules:
  0.0 47.3 jit_solution(8930458792278903883)
XLA Ops:
  0.0 45.3 %forecast.1 = f32[512,2048]{1,0:T(8,128)S(1)} custom-call(f32[512,2048]{1,0:T(8,128)} %cov.1, f32[128,128]{1,0:T(8,128)} %lon_hbm.1, f32[128,128]{1,0:T(8,128)} %lat_hbm.1, s32[128,128]{1,0:T(8,128)} %zonal_hbm.1, s32[128,128]{1,0:T(8,128)} %sign_hbm.1, s32[128]{0:T(128)} %counts_hbm.1), custom_call_target="tpu_custom_call" | custom-call | tf_op jit(solution)/shard_map/forecast/pallas_call | solution.py:386
  45.3 2.0 %copy.8 = f32[512,2048]{1,0:T(8,128)} copy(f32[512,2048]{1,0:T(8,128)S(1)} %forecast.1) | data formatting | bytes 8388608

commit v3 on v2

--- a/solution.py
+++ b/solution.py
@@ -12,7 +12,8 @@
 NLON = 128
 SUBCYCLES = 4
 WIDE = 256
-RELAYED = (5, 6, 8, 9)
+RELAYS = {4: (31, 0), 5: (31, 0), 6: (19, 12), 7: (21, 10), 8: (28, 3), 9: (26, 5)}
+RELAY_TURN = {4: 1, 5: 2, 6: 1, 7: 2, 8: 1, 9: 2}
 F32 = jnp.float32
 BF16 = jnp.bfloat16
 
@@ -69,17 +70,15 @@
 
     half = rows_n // 2
     below_gap, above_gap = r == half - 1, r == half
-    bottom, top = r == 0, r == rows_n - 1
-    via_top = (rows_n - 1, c)
-    via_bottom = (0, c)
     to_below_gap, to_above_gap = (half - 1, c), (half, c)
 
     barrier = pltpu.get_barrier_semaphore()
-    links = (
-        (has_down, down), (has_up, up), (has_left, left), (has_right, right),
-        (below_gap, via_top), (top, to_below_gap), (top, to_above_gap), (above_gap, via_top),
-        (above_gap, via_bottom), (bottom, to_above_gap), (bottom, to_below_gap), (below_gap, via_bottom),
-    )
+    links = [(has_down, down), (has_up, up), (has_left, left), (has_right, right)]
+    for relay in sorted({relay for pair in RELAYS.values() for relay in pair}):
+        links += [
+            (below_gap, (relay, c)), (above_gap, (relay, c)),
+            (r == relay, to_below_gap), (r == relay, to_above_gap),
+        ]
     for exists, device in links:
         @pl.when(exists)
         def _():
@@ -126,7 +125,7 @@
         return pltpu.make_async_remote_copy(
             cov.at[pl.ds(rows - halo if rising else 0, halo), at], relayed.at[:, at],
             row_send.at[int(rising), piece], relay_recv.at[piece],
-            device_id=via_top if rising else via_bottom, device_id_type=MESH,
+            device_id=(RELAYS[piece][0 if rising else 1], c), device_id_type=MESH,
         )
 
     def from_relay(piece, at, rising):
@@ -139,7 +138,7 @@
     order = (0, 3, 1, 2, *range(4, 4 + inner))
     for piece in order:
         at = piece_columns(piece)
-        if piece in RELAYED:
+        if piece in RELAYS:
             @pl.when(above_gap)
             def _():
                 to_relay(piece, at, False).start()
@@ -279,16 +278,13 @@
             col_send.at[1, lat], col_recv.at[1, lat], device_id=right, device_id_type=MESH,
         )
 
-    def pass_on(piece, at):
-        @pl.when(top)
-        def _():
-            to_relay(piece, at, True).wait_recv()
-            from_relay(piece, at, True).start()
-
-        @pl.when(bottom)
-        def _():
-            to_relay(piece, at, False).wait_recv()
-            from_relay(piece, at, False).start()
+    def pass_on(piece):
+        at = piece_columns(piece)
+        for relay, rising in zip(RELAYS[piece], (True, False)):
+            @pl.when(r == relay)
+            def _():
+                to_relay(piece, at, rising).wait_recv()
+                from_relay(piece, at, rising).start()
 
     load.wait()
     for piece in (0, 3, 1, 2):
@@ -306,11 +302,12 @@
     lax.fori_loop(0, col_lats + 2, prepare_col, 0)
 
     def interior(chunk, carry):
-        goes_on = functools.reduce(jnp.logical_or, [chunk == piece - 4 for piece in RELAYED])
-
-        @pl.when(goes_on)
-        def _():
-            pass_on(4 + chunk, inner_columns(chunk))
+        for turn in sorted(set(RELAY_TURN.values())):
+            @pl.when(chunk == turn)
+            def _():
+                for piece in RELAYS:
+                    if RELAY_TURN[piece] == turn:
+                        pass_on(piece)
 
         row_chunk(4 + chunk, pl.multiple_of((chunk + 1) * WIDE, WIDE), WIDE)
         col_middle(2 * chunk + 2)
@@ -360,10 +357,11 @@
         def _():
             to_up(piece, at).wait_send()
 
-        if piece in RELAYED:
-            @pl.when(jnp.logical_or(top, bottom))
-            def _():
-                from_relay(piece, at, True).wait_send()
+        if piece in RELAYS:
+            for relay, rising in zip(RELAYS[piece], (True, False)):
+                @pl.when(r == relay)
+                def _():
+                    from_relay(piece, at, rising).wait_send()
 
     for lat in range(2):
         @pl.when(has_left)

time: 47.4 us -> 42.6 us (0.90); the launches traced: 47.3 us -> 41.9 us
  Pallas kernels: 45.3 us -> 39.9 us
    pallas_call x1, Pallas kernels: 45.3 us -> 39.9 us  [per_device(): pl.pallas_call(functools.partial(kernel, rows_n, cols_n), out_shape=jax.S...]
where the time goes in v3:
time: 42.6 us; the launch traced here: 41.9 us
  Pallas kernels  39.9 us (94%)
  local copies, waits for them, and re-layouts  2.02 us (5%)
    pallas_call x1, Pallas kernels, per_device(): pl.pallas_call(functools.partial(kernel, rows_n, cols_n), out_shape=jax.S...  39.9 us
    unnamed x1, local copies, waits for them, and re-layouts  2.02 us

profile of v3, /device:TPU:9, one launch (start us, length us, event | category | flops | bytes accessed | tf_op | source)
XLA Modules:
  0.0 41.9 jit_solution(12821717051713887780)
XLA Ops:
  0.0 39.9 %forecast.1 = f32[512,2048]{1,0:T(8,128)S(1)} custom-call(f32[512,2048]{1,0:T(8,128)} %cov.1, f32[128,128]{1,0:T(8,128)} %lon_hbm.1, f32[128,128]{1,0:T(8,128)} %lat_hbm.1, s32[128,128]{1,0:T(8,128)} %zonal_hbm.1, s32[128,128]{1,0:T(8,128)} %sign_hbm.1, s32[128]{0:T(128)} %counts_hbm.1), custom_call_target="tpu_custom_call" | custom-call | tf_op jit(solution)/shard_map/forecast/pallas_call | solution.py:384
  39.9 2.0 %copy.8 = f32[512,2048]{1,0:T(8,128)} copy(f32[512,2048]{1,0:T(8,128)S(1)} %forecast.1) | data formatting | bytes 8388608

commit v4 on v3

--- a/solution.py
+++ b/solution.py
@@ -11,9 +11,10 @@
 NLAT = 128
 NLON = 128
 SUBCYCLES = 4
+EDGE_LATS = (-1, 0, 1, 14, 15, 16)
 WIDE = 256
-RELAYS = {4: (31, 0), 5: (31, 0), 6: (19, 12), 7: (21, 10), 8: (28, 3), 9: (26, 5)}
-RELAY_TURN = {4: 1, 5: 2, 6: 1, 7: 2, 8: 1, 9: 2}
+RELAYS = {4: (31, 12), 5: (31, 12), 6: (19, 10), 7: (21, 3), 8: (28, 5), 9: (26, 7), 10: (26, None)}
+RELAY_TURN = {4: 1, 5: 1, 6: 1, 7: 2, 8: 1, 9: 2, 10: 2}
 F32 = jnp.float32
 BF16 = jnp.bfloat16
 
@@ -51,17 +52,18 @@
 def kernel(
     rows_n, cols_n,
     cov, lon_hbm, lat_hbm, zonal_hbm, sign_hbm, counts_hbm,
-    final,
-    ext, wide, relayed, row_mid, col_mid,
+    final, wide, col_mid, col_hi, col_lo, edge_rows,
+    ext, relayed, row_mid,
     lon_ref, lat_ref, zonal_ref, sign_ref, counts_ref,
-    row_rate, row_sign, row_hi, row_lo, col_hi, col_lo,
+    row_rate, row_sign, row_hi, row_lo,
     load_sem, table_sem, row_send, row_recv, relay_recv, relay_send, col_send, col_recv,
 ):
     r, c = lax.axis_index("row"), lax.axis_index("col")
     rows, cols = cov.shape
     row_lats, col_lats = rows // NLON, cols // NLON
     halo = 2 * NLON
-    inner = cols // WIDE - 2
+    inner = cols // WIDE - 3
+    pieces = inner + 6
     first_row, first_col = r * row_lats, c * col_lats
     has_down, has_up = r > 0, r < rows_n - 1
     has_left, has_right = c > 0, c < cols_n - 1
@@ -74,7 +76,7 @@
 
     barrier = pltpu.get_barrier_semaphore()
     links = [(has_down, down), (has_up, up), (has_left, left), (has_right, right)]
-    for relay in sorted({relay for pair in RELAYS.values() for relay in pair}):
+    for relay in sorted({relay for pair in RELAYS.values() for relay in pair if relay is not None}):
         links += [
             (below_gap, (relay, c)), (above_gap, (relay, c)),
             (r == relay, to_below_gap), (r == relay, to_above_gap),
@@ -102,7 +104,11 @@
         if piece < 4:
             lat = (0, 1, col_lats - 2, col_lats - 1)[piece]
             return pl.ds(lat * NLON, NLON)
-        return inner_columns(piece - 4)
+        if piece < 4 + inner:
+            return inner_columns(piece - 4)
+        return pl.ds(inner_end + (piece - 4 - inner) * NLON, NLON)
+
+    inner_end = (inner + 1) * WIDE
 
     def inner_columns(chunk):
         return pl.ds(pl.multiple_of((chunk + 1) * WIDE, WIDE), WIDE)
@@ -135,33 +141,26 @@
             device_id=to_above_gap if rising else to_below_gap, device_id_type=MESH,
         )
 
-    order = (0, 3, 1, 2, *range(4, 4 + inner))
+    order = (0, 3, 1, 2, *range(4, pieces))
     for piece in order:
         at = piece_columns(piece)
-        if piece in RELAYS:
-            @pl.when(above_gap)
-            def _():
-                to_relay(piece, at, False).start()
-
-            @pl.when(below_gap)
-            def _():
-                to_relay(piece, at, True).start()
-
-            @pl.when(jnp.logical_and(has_down, jnp.logical_not(above_gap)))
-            def _():
-                to_down(piece, at).start()
-
-            @pl.when(jnp.logical_and(has_up, jnp.logical_not(below_gap)))
-            def _():
-                to_up(piece, at).start()
-        else:
-            @pl.when(has_down)
-            def _():
-                to_down(piece, at).start()
-
-            @pl.when(has_up)
-            def _():
-                to_up(piece, at).start()
+        by_top, by_bottom = RELAYS.get(piece, (None, None))
+        for relay, rising, gap, exists, direct in (
+            (by_bottom, False, above_gap, has_down, to_down),
+            (by_top, True, below_gap, has_up, to_up),
+        ):
+            if relay is None:
+                @pl.when(exists)
+                def _():
+                    direct(piece, at).start()
+            else:
+                @pl.when(gap)
+                def _():
+                    to_relay(piece, at, rising).start()
+
+                @pl.when(jnp.logical_and(exists, jnp.logical_not(gap)))
+                def _():
+                    direct(piece, at).start()
 
     @pl.when(jnp.logical_not(has_down))
     def _():
@@ -201,7 +200,7 @@
         row_lo[i] = low
         return carry
 
-    lax.fori_loop(0, row_lats + 2, prepare_row, 0)
+    lax.fori_loop(0, row_lats + 2, prepare_row, 0, unroll=3)
 
     def prepare_col(i, carry):
         at = clamped(first_col - 1 + i)
@@ -281,6 +280,9 @@
     def pass_on(piece):
         at = piece_columns(piece)
         for relay, rising in zip(RELAYS[piece], (True, False)):
+            if relay is None:
+                continue
+
             @pl.when(r == relay)
             def _():
                 to_relay(piece, at, rising).wait_recv()
@@ -289,6 +291,8 @@
     load.wait()
     for piece in (0, 3, 1, 2):
         lat = (0, 1, col_lats - 2, col_lats - 1)[piece]
+        if piece in RELAYS:
+            pass_on(piece)
         row_chunk(piece, lat * NLON, NLON)
         if piece < 2:
             @pl.when(has_left)
@@ -299,13 +303,13 @@
             def _():
                 to_right(piece - 2).start()
 
-    lax.fori_loop(0, col_lats + 2, prepare_col, 0)
+    lax.fori_loop(0, col_lats + 2, prepare_col, 0, unroll=3)
 
     def interior(chunk, carry):
         for turn in sorted(set(RELAY_TURN.values())):
             @pl.when(chunk == turn)
             def _():
-                for piece in RELAYS:
+                for piece in RELAY_TURN:
                     if RELAY_TURN[piece] == turn:
                         pass_on(piece)
 
@@ -321,9 +325,20 @@
         return carry
 
     lax.fori_loop(0, inner, interior, 0)
-    col_middle(2 * inner + 2)
-    col_middle(2 * inner + 3)
-    for k in range(2 * inner, 2 * inner + 2):
+
+    for i, lat in enumerate(EDGE_LATS):
+        edge_rows[pl.ds(i, 1), :] = courant_of(first_col + lat)
+        edge_rows[pl.ds(8 + i, 1), :] = sign_ref[
+            pl.ds(clamped(first_col + lat), 1), :
+        ].astype(F32)
+
+    row_chunk(pieces - 2, inner_end, NLON)
+    col_middle(col_lats - 4)
+    col_final(col_lats - 6)
+    row_chunk(pieces - 1, inner_end + NLON, NLON)
+    for i in range(col_lats - 3, col_lats):
+        col_middle(i)
+    for k in range(col_lats - 5, col_lats - 2):
         col_final(k)
 
     @pl.when(has_right)
@@ -331,21 +346,11 @@
         to_left(0).wait_recv()
         to_left(1).wait_recv()
 
-    col_middle(col_lats)
-    col_middle(col_lats + 1)
-    col_final(col_lats - 2)
-    col_final(col_lats - 1)
-
     @pl.when(has_left)
     def _():
         to_right(0).wait_recv()
         to_right(1).wait_recv()
 
-    col_middle(0)
-    col_middle(1)
-    col_final(0)
-    col_final(1)
-
     for piece in order:
         at = piece_columns(piece)
 
@@ -359,6 +364,9 @@
 
         if piece in RELAYS:
             for relay, rising in zip(RELAYS[piece], (True, False)):
+                if relay is None:
+                    continue
+
                 @pl.when(r == relay)
                 def _():
                     from_relay(piece, at, rising).wait_send()
@@ -373,25 +381,77 @@
             to_right(lat).wait_send()
 
 
+def finish(
+    final, wide, col_mid, col_hi, col_lo, edge_rows, out, edge_mid, edge_final, sems
+):
+    rows, cols = final.shape
+    col_lats = cols // NLON
+    edge = 2 * NLON
+    inner = pl.ds(edge, cols - 2 * edge)
+    stores = [pltpu.make_async_copy(final.at[:, inner], out.at[:, inner], sems.at[0])]
+    stores[0].start()
+
+    def lat_columns(index):
+        return pl.ds(index * NLON, NLON)
+
+    def row_of(lat):
+        at = EDGE_LATS.index(lat)
+        return edge_rows[pl.ds(at, 1), :], edge_rows[pl.ds(8 + at, 1), :] == 1.0
+
+    def middle(lat):
+        moved = upwind(
+            wide[:, lat_columns(lat + 2)], wide[:, lat_columns(lat + 1)],
+            wide[:, lat_columns(lat + 3)], *row_of(lat),
+        )
+        high, low = split(moved)
+        i = lat + 1
+        return dot(high, col_hi[i]) + (dot(low, col_hi[i]) + dot(high, col_lo[i]))
+
+    for side, (outer, near) in enumerate((((-1, 0), (1, 2)), ((col_lats, col_lats - 1), (col_lats - 2, col_lats - 3)))):
+        for at, lat in enumerate(outer):
+            edge_mid[side, at] = middle(lat)
+        mids = {lat: edge_mid[side, at] for at, lat in enumerate(outer)}
+        mids |= {lat: col_mid[:, lat_columns(lat + 1)] for lat in near}
+        first = 0 if side == 0 else cols - edge
+        for lat in (outer[1], near[0]):
+            place = lat * NLON - first
+            edge_final[side, :, pl.ds(place, NLON)] = upwind(
+                mids[lat], mids[lat - 1], mids[lat + 1], *row_of(lat)
+            )
+        store = pltpu.make_async_copy(
+            edge_final.at[side], out.at[:, pl.ds(first, edge)], sems.at[1 + side]
+        )
+        store.start()
+        stores.append(store)
+    for store in stores:
+        store.wait()
+
+
 def solution(mesh):
     rows_n, cols_n = mesh.shape["row"], mesh.shape["col"]
 
     def per_device(covariance, lon_courant, lat_courant, zonal_upwind_sign, lat_sign, cycle_counts):
         rows, cols = covariance.shape
         row_lats, col_lats = rows // NLON, cols // NLON
-        pieces = cols // WIDE + 2
+        pieces = cols // WIDE + 3
         hbm = pl.BlockSpec(memory_space=pltpu.HBM)
-        return pl.pallas_call(
+        vmem = pl.BlockSpec(memory_space=pltpu.VMEM)
+        parts = pl.pallas_call(
             functools.partial(kernel, rows_n, cols_n),
-            out_shape=jax.ShapeDtypeStruct((rows, cols), F32),
+            out_shape=[
+                jax.ShapeDtypeStruct((rows, cols), F32),
+                jax.ShapeDtypeStruct((rows, cols + 4 * NLON), F32),
+                jax.ShapeDtypeStruct((rows, cols + 2 * NLON), F32),
+                jax.ShapeDtypeStruct((col_lats + 2, NLON, NLON), BF16),
+                jax.ShapeDtypeStruct((col_lats + 2, NLON, NLON), BF16),
+                jax.ShapeDtypeStruct((16, NLON), F32),
+            ],
             in_specs=[hbm] * 6,
-            out_specs=pl.BlockSpec(memory_space=pltpu.VMEM),
+            out_specs=[vmem] * 6,
             scratch_shapes=[
                 pltpu.VMEM((rows + 4 * NLON, cols), F32),
-                pltpu.VMEM((rows, cols + 4 * NLON), F32),
                 pltpu.VMEM((2 * NLON, cols), F32),
                 pltpu.VMEM((row_lats + 2, NLON, WIDE), F32),
-                pltpu.VMEM((rows, cols + 2 * NLON), F32),
                 pltpu.VMEM((NLAT, NLON), F32),
                 pltpu.VMEM((NLAT, NLON), F32),
                 pltpu.VMEM((NLAT, NLON), jnp.int32),
@@ -401,8 +461,6 @@
                 pltpu.VMEM((row_lats + 2, NLON, NLON), F32),
                 pltpu.VMEM((row_lats + 2, NLON, NLON), BF16),
                 pltpu.VMEM((row_lats + 2, NLON, NLON), BF16),
-                pltpu.VMEM((col_lats + 2, NLON, NLON), BF16),
-                pltpu.VMEM((col_lats + 2, NLON, NLON), BF16),
                 pltpu.SemaphoreType.DMA,
                 pltpu.SemaphoreType.DMA((5,)),
                 pltpu.SemaphoreType.DMA((2, pieces)),
@@ -414,9 +472,22 @@
             ],
             name="forecast",
             compiler_params=pltpu.CompilerParams(
-                collective_id=0, has_side_effects=True, vmem_limit_bytes=48 * 2**20
+                collective_id=0, has_side_effects=True, vmem_limit_bytes=36 * 2**20
             ),
         )(*[pltpu.with_memory_space_constraint(a, pltpu.HBM) for a in (covariance, lon_courant, lat_courant, zonal_upwind_sign, lat_sign, cycle_counts)])
+        return pl.pallas_call(
+            finish,
+            out_shape=jax.ShapeDtypeStruct((rows, cols), F32),
+            in_specs=[vmem] * 6,
+            out_specs=hbm,
+            scratch_shapes=[
+                pltpu.VMEM((2, 2, rows, NLON), F32),
+                pltpu.VMEM((2, rows, 2 * NLON), F32),
+                pltpu.SemaphoreType.DMA((3,)),
+            ],
+            name="finish",
+            compiler_params=pltpu.CompilerParams(vmem_limit_bytes=36 * 2**20),
+        )(*parts)
 
     placed = (P("row", "col"), P(), P(), P(), P(), P())
     return jax.shard_map(

time: 42.6 us -> 41.6 us (0.977)
  the two profiles are of different devices: /device:TPU:9 before, /device:TPU:233 now
where the time goes in v4:
time: 41.6 us
  Pallas kernels  41.5 us (100%)
    pallas_call x1, Pallas kernels, per_device(): pl.pallas_call(functools.partial(kernel, rows_n, cols_n), out_shape=[jax....  39.5 us
    pallas_call x1, Pallas kernels, per_device(): pl.pallas_call(finish, out_shape=jax.ShapeDtypeStruct((rows, cols), F32),...  2.04 us

profile of v4, /device:TPU:233, one launch (start us, length us, event | category | flops | bytes accessed | tf_op | source)
XLA Modules:
  0.0 41.6 jit_solution(2007109435900853671)
XLA Ops:
  0.0 39.5 %forecast.1 = (f32[512,2048]{1,0:T(8,128)S(1)}, f32[512,2560]{1,0:T(8,128)S(1)}, f32[512,2304]{1,0:T(8,128)S(1)}, bf16[18,128,128]{2,1,0:T(8,128)(2,1)S(1)}, bf1...) custom-call(f32[512,2048]{1,0:T(8,128)} %cov.1, f32[128,128]{1,0:T(8,128)} %lon_hbm.1, f32[128,128]{1,0:T(8,128)} %lat_hbm.1, ...), custom_call_target="tpu_custom_call" | custom-call | tf_op jit(solution)/shard_map/forecast/pallas_call | solution.py:439
  39.5 2.0 %finish.1 = f32[512,2048]{1,0:T(8,128)} custom-call(f32[512,2048]{1,0:T(8,128)S(1)} %get-tuple-element.11.final, f32[512,2560]{1,0:T(8,128)S(1)} %get-tuple-element.12.wide, f32[512,2304]{1,0:T(8,128)S(1)} %get-tuple-element.13.col_mid, bf16[18,128,128]{2,1,0:T(8,128)(2,1)S(1)} %get-tuple-element.14.col_hi, ...), custom_call_target="tpu_custom_call" | custom-call | tf_op jit(solution)/shard_map/finish/pallas_call | solution.py:478

commit v5 on v4

--- a/solution.py
+++ b/solution.py
@@ -13,8 +13,8 @@
 SUBCYCLES = 4
 EDGE_LATS = (-1, 0, 1, 14, 15, 16)
 WIDE = 256
-RELAYS = {4: (31, 12), 5: (31, 12), 6: (19, 10), 7: (21, 3), 8: (28, 5), 9: (26, 7), 10: (26, None)}
-RELAY_TURN = {4: 1, 5: 1, 6: 1, 7: 2, 8: 1, 9: 2, 10: 2}
+RELAYS = {1: (31, None), 4: (31, 0), 5: (31, 12), 6: (19, 10), 7: (21, 3), 8: (28, 5), 9: (26, 0), 10: (26, None)}
+RELAY_TURN = {4: 1, 5: 1, 6: 1, 7: 2, 8: 1, 9: 1, 10: 2}
 F32 = jnp.float32
 BF16 = jnp.bfloat16
 
@@ -53,7 +53,7 @@
     rows_n, cols_n,
     cov, lon_hbm, lat_hbm, zonal_hbm, sign_hbm, counts_hbm,
     final, wide, col_mid, col_hi, col_lo, edge_rows,
-    ext, relayed, row_mid,
+    ext, relayed, row_mid, edge_row_mid,
     lon_ref, lat_ref, zonal_ref, sign_ref, counts_ref,
     row_rate, row_sign, row_hi, row_lo,
     load_sem, table_sem, row_send, row_recv, relay_recv, relay_send, col_send, col_recv,
@@ -263,19 +263,72 @@
             col_mid[:, lat_columns(k + 2)], courant_of(lat), from_below,
         )
 
-    def to_left(lat):
+    core = lax.rem(r, 2)
+
+    def half_rows(late):
+        part = core if late else 1 - core
+        return pl.ds(pl.multiple_of(part * (rows // 2), rows // 2), rows // 2)
+
+    def to_left(lat, late):
+        at = half_rows(late)
         return pltpu.make_async_remote_copy(
-            wide.at[:, pl.ds(halo + lat * NLON, NLON)],
-            wide.at[:, pl.ds(halo + cols + lat * NLON, NLON)],
-            col_send.at[0, lat], col_recv.at[0, lat], device_id=left, device_id_type=MESH,
-        )
-
-    def to_right(lat):
+            wide.at[at, pl.ds(halo + lat * NLON, NLON)],
+            wide.at[at, pl.ds(halo + cols + lat * NLON, NLON)],
+            col_send.at[0, 2 * lat + late], col_recv.at[0, 2 * lat + late],
+            device_id=left, device_id_type=MESH,
+        )
+
+    def to_right(lat, late):
+        at = half_rows(late)
         return pltpu.make_async_remote_copy(
-            wide.at[:, pl.ds(cols + lat * NLON, NLON)],
-            wide.at[:, pl.ds(lat * NLON, NLON)],
-            col_send.at[1, lat], col_recv.at[1, lat], device_id=right, device_id_type=MESH,
-        )
+            wide.at[at, pl.ds(cols + lat * NLON, NLON)],
+            wide.at[at, pl.ds(lat * NLON, NLON)],
+            col_send.at[1, 2 * lat + late], col_recv.at[1, 2 * lat + late],
+            device_id=right, device_id_type=MESH,
+        )
+
+    def edge_half(piece, late):
+        start = (0, 1, col_lats - 2, col_lats - 1)[piece] * NLON
+        at = pl.ds(start, NLON)
+
+        @pl.when(jnp.logical_and(core == late, has_up))
+        def _():
+            to_down(piece, at).wait_recv()
+
+        @pl.when(jnp.logical_and(core != late, has_down))
+        def _():
+            to_up(piece, at).wait_recv()
+
+        def lat_rows(index):
+            return pl.ds(pl.multiple_of(index * NLON, NLON), NLON)
+
+        upper = 1 - core
+        first = 4 - 4 * upper if late else 2 * upper
+        for step in range(2 if late else 4):
+            i = first + step
+            moved = upwind(
+                ext[lat_rows(i + 1), at], ext[lat_rows(i), at], ext[lat_rows(i + 2), at],
+                row_rate[i], row_sign[i] == 1.0,
+            )
+            high, low = split(moved)
+            edge_row_mid[piece, i] = (
+                dot(row_hi[i], high) + (dot(row_hi[i], low) + dot(row_lo[i], high))
+            )
+        first = 2 - 2 * upper if late else 2 * upper
+        for step in range(1, 3):
+            i = first + step
+            wide[lat_rows(i - 1), pl.ds(halo + start, NLON)] = upwind(
+                edge_row_mid[piece, i], edge_row_mid[piece, i - 1], edge_row_mid[piece, i + 1],
+                row_rate[i], row_sign[i] == 1.0,
+            )
+        if piece < 2:
+            @pl.when(has_left)
+            def _():
+                to_left(piece, late).start()
+        else:
+            @pl.when(has_right)
+            def _():
+                to_right(piece - 2, late).start()
 
     def pass_on(piece):
         at = piece_columns(piece)
@@ -289,19 +342,11 @@
                 from_relay(piece, at, rising).start()
 
     load.wait()
-    for piece in (0, 3, 1, 2):
-        lat = (0, 1, col_lats - 2, col_lats - 1)[piece]
-        if piece in RELAYS:
-            pass_on(piece)
-        row_chunk(piece, lat * NLON, NLON)
-        if piece < 2:
-            @pl.when(has_left)
-            def _():
-                to_left(piece).start()
-        else:
-            @pl.when(has_right)
-            def _():
-                to_right(piece - 2).start()
+    for late in range(2):
+        for piece in (0, 3, 1, 2):
+            if late and piece in RELAYS:
+                pass_on(piece)
+            edge_half(piece, late)
 
     lax.fori_loop(0, col_lats + 2, prepare_col, 0, unroll=3)
 
@@ -343,13 +388,15 @@
 
     @pl.when(has_right)
     def _():
-        to_left(0).wait_recv()
-        to_left(1).wait_recv()
+        for lat in range(2):
+            for late in range(2):
+                to_left(lat, late).wait_recv()
 
     @pl.when(has_left)
     def _():
-        to_right(0).wait_recv()
-        to_right(1).wait_recv()
+        for lat in range(2):
+            for late in range(2):
+                to_right(lat, late).wait_recv()
 
     for piece in order:
         at = piece_columns(piece)
@@ -372,13 +419,14 @@
                     from_relay(piece, at, rising).wait_send()
 
     for lat in range(2):
-        @pl.when(has_left)
-        def _():
-            to_left(lat).wait_send()
-
-        @pl.when(has_right)
-        def _():
-            to_right(lat).wait_send()
+        for late in range(2):
+            @pl.when(has_left)
+            def _():
+                to_left(lat, late).wait_send()
+
+            @pl.when(has_right)
+            def _():
+                to_right(lat, late).wait_send()
 
 
 def finish(
@@ -452,6 +500,7 @@
                 pltpu.VMEM((rows + 4 * NLON, cols), F32),
                 pltpu.VMEM((2 * NLON, cols), F32),
                 pltpu.VMEM((row_lats + 2, NLON, WIDE), F32),
+                pltpu.VMEM((4, row_lats + 2, NLON, NLON), F32),
                 pltpu.VMEM((NLAT, NLON), F32),
                 pltpu.VMEM((NLAT, NLON), F32),
                 pltpu.VMEM((NLAT, NLON), jnp.int32),
@@ -467,8 +516,8 @@
                 pltpu.SemaphoreType.DMA((2, pieces)),
                 pltpu.SemaphoreType.DMA((pieces,)),
                 pltpu.SemaphoreType.DMA((pieces,)),
-                pltpu.SemaphoreType.DMA((2, 2)),
-                pltpu.SemaphoreType.DMA((2, 2)),
+                pltpu.SemaphoreType.DMA((2, 4)),
+                pltpu.SemaphoreType.DMA((2, 4)),
             ],
             name="forecast",
             compiler_params=pltpu.CompilerParams(

time: 41.6 us -> 40.8 us (0.981)
  the two profiles are of different devices: /device:TPU:233 before, /device:TPU:9 now
where the time goes in v5:
time: 40.8 us; the launch traced here: 40.1 us
  Pallas kernels  40.1 us (98%)
    pallas_call x1, Pallas kernels, per_device(): pl.pallas_call(functools.partial(kernel, rows_n, cols_n), out_shape=[jax....  38.1 us
    pallas_call x1, Pallas kernels, per_device(): pl.pallas_call(finish, out_shape=jax.ShapeDtypeStruct((rows, cols), F32),...  2.04 us

profile of v5, /device:TPU:9, one launch (start us, length us, event | category | flops | bytes accessed | tf_op | source)
XLA Modules:
  0.0 40.1 jit_solution(13298631855722854003)
XLA Ops:
  0.0 38.1 %forecast.1 = (f32[512,2048]{1,0:T(8,128)S(1)}, f32[512,2560]{1,0:T(8,128)S(1)}, f32[512,2304]{1,0:T(8,128)S(1)}, bf16[18,128,128]{2,1,0:T(8,128)(2,1)S(1)}, bf1...) custom-call(f32[512,2048]{1,0:T(8,128)} %cov.1, f32[128,128]{1,0:T(8,128)} %lon_hbm.1, f32[128,128]{1,0:T(8,128)} %lat_hbm.1, ...), custom_call_target="tpu_custom_call" | custom-call | tf_op jit(solution)/shard_map/forecast/pallas_call | solution.py:487
  38.1 2.0 %finish.1 = f32[512,2048]{1,0:T(8,128)} custom-call(f32[512,2048]{1,0:T(8,128)S(1)} %get-tuple-element.11.final, f32[512,2560]{1,0:T(8,128)S(1)} %get-tuple-element.12.wide, f32[512,2304]{1,0:T(8,128)S(1)} %get-tuple-element.13.col_mid, bf16[18,128,128]{2,1,0:T(8,128)(2,1)S(1)} %get-tuple-element.14.col_hi, ...), custom_call_target="tpu_custom_call" | custom-call | tf_op jit(solution)/shard_map/finish/pallas_call | solution.py:527

commit v6 on v5

--- a/solution.py
+++ b/solution.py
@@ -81,10 +81,20 @@
             (below_gap, (relay, c)), (above_gap, (relay, c)),
             (r == relay, to_below_gap), (r == relay, to_above_gap),
         ]
-    for exists, device in links:
-        @pl.when(exists)
-        def _():
-            pl.semaphore_signal(barrier, inc=1, device_id=device, device_id_type=MESH)
+    def greet(pairs):
+        for exists, device in pairs:
+            @pl.when(exists)
+            def _():
+                pl.semaphore_signal(barrier, inc=1, device_id=device, device_id_type=MESH)
+
+    near = 4
+    relaying = functools.reduce(jnp.logical_or, [exists for exists, _ in links[near:]])
+
+    @pl.when(relaying)
+    def _():
+        greet(links[near:])
+
+    greet(links[:near])
 
     tables = [
         pltpu.make_async_copy(source, target, table_sem.at[i])

time: 40.8 us -> 40.9 us (level)
  no operation moved by 1% of the time
where the time goes in v6:
time: 40.9 us; the launch traced here: 40.1 us
  Pallas kernels  40.1 us (98%)
    pallas_call x1, Pallas kernels, per_device(): pl.pallas_call(functools.partial(kernel, rows_n, cols_n), out_shape=[jax....  38.1 us
    pallas_call x1, Pallas kernels, per_device(): pl.pallas_call(finish, out_shape=jax.ShapeDtypeStruct((rows, cols), F32),...  2.04 us

profile of v6, /device:TPU:9, one launch (start us, length us, event | category | flops | bytes accessed | tf_op | source)
XLA Modules:
  0.0 40.1 jit_solution(16644822523540039927)
XLA Ops:
  0.0 38.1 %forecast.1 = (f32[512,2048]{1,0:T(8,128)S(1)}, f32[512,2560]{1,0:T(8,128)S(1)}, f32[512,2304]{1,0:T(8,128)S(1)}, bf16[18,128,128]{2,1,0:T(8,128)(2,1)S(1)}, bf1...) custom-call(f32[512,2048]{1,0:T(8,128)} %cov.1, f32[128,128]{1,0:T(8,128)} %lon_hbm.1, f32[128,128]{1,0:T(8,128)} %lat_hbm.1, ...), custom_call_target="tpu_custom_call" | custom-call | tf_op jit(solution)/shard_map/forecast/pallas_call | solution.py:497
  38.1 2.0 %finish.1 = f32[512,2048]{1,0:T(8,128)} custom-call(f32[512,2048]{1,0:T(8,128)S(1)} %get-tuple-element.11.final, f32[512,2560]{1,0:T(8,128)S(1)} %get-tuple-element.12.wide, f32[512,2304]{1,0:T(8,128)S(1)} %get-tuple-element.13.col_mid, bf16[18,128,128]{2,1,0:T(8,128)(2,1)S(1)} %get-tuple-element.14.col_hi, ...), custom_call_target="tpu_custom_call" | custom-call | tf_op jit(solution)/shard_map/finish/pallas_call | solution.py:537

commit v7 on v6

--- a/solution.py
+++ b/solution.py
@@ -152,7 +152,7 @@
         )
 
     order = (0, 3, 1, 2, *range(4, pieces))
-    for piece in order:
+    def send_piece(piece):
         at = piece_columns(piece)
         by_top, by_bottom = RELAYS.get(piece, (None, None))
         for relay, rising, gap, exists, direct in (
@@ -172,6 +172,9 @@
                 def _():
                     direct(piece, at).start()
 
+    for piece in order[:4]:
+        send_piece(piece)
+
     @pl.when(jnp.logical_not(has_down))
     def _():
         ext[pl.ds(0, halo), :] = jnp.zeros((halo, cols), F32)
@@ -211,6 +214,9 @@
         return carry
 
     lax.fori_loop(0, row_lats + 2, prepare_row, 0, unroll=3)
+
+    for piece in order[4:]:
+        send_piece(piece)
 
     def prepare_col(i, carry):
         at = clamped(first_col - 1 + i)

time: 40.9 us -> 41.7 us (1.020)
  the two profiles are of different devices: /device:TPU:9 before, /device:TPU:26 now
where the time goes in v7:
time: 41.7 us; the launch traced here: 41.6 us
  Pallas kernels  41.6 us (100%)
    pallas_call x1, Pallas kernels, per_device(): pl.pallas_call(functools.partial(kernel, rows_n, cols_n), out_shape=[jax....  39.6 us
    pallas_call x1, Pallas kernels, per_device(): pl.pallas_call(finish, out_shape=jax.ShapeDtypeStruct((rows, cols), F32),...  2.04 us

profile of v7, /device:TPU:26, one launch (start us, length us, event | category | flops | bytes accessed | tf_op | source)
XLA Modules:
  0.0 41.6 jit_solution(12732899739317162436)
XLA Ops:
  0.0 39.6 %forecast.1 = (f32[512,2048]{1,0:T(8,128)S(1)}, f32[512,2560]{1,0:T(8,128)S(1)}, f32[512,2304]{1,0:T(8,128)S(1)}, bf16[18,128,128]{2,1,0:T(8,128)(2,1)S(1)}, bf1...) custom-call(f32[512,2048]{1,0:T(8,128)} %cov.1, f32[128,128]{1,0:T(8,128)} %lon_hbm.1, f32[128,128]{1,0:T(8,128)} %lat_hbm.1, ...), custom_call_target="tpu_custom_call" | custom-call | tf_op jit(solution)/shard_map/forecast/pallas_call | solution.py:503
  39.6 2.0 %finish.1 = f32[512,2048]{1,0:T(8,128)} custom-call(f32[512,2048]{1,0:T(8,128)S(1)} %get-tuple-element.11.final, f32[512,2560]{1,0:T(8,128)S(1)} %get-tuple-element.12.wide, f32[512,2304]{1,0:T(8,128)S(1)} %get-tuple-element.13.col_mid, bf16[18,128,128]{2,1,0:T(8,128)(2,1)S(1)} %get-tuple-element.14.col_hi, ...), custom_call_target="tpu_custom_call" | custom-call | tf_op jit(solution)/shard_map/finish/pallas_call | solution.py:543
